TPU v7x, 32 devices: a whole 2x2x4 slice. The times are simulated.
32 devices in a mesh: tm: 16 (over z, y, x), ens: 2 (over core).
Axes of the slice: x: 2, y: 2, z: 4, core: 2. Of those that a mesh axis runs over, the one named last changes fastest.
Arguments:
- drift_raw: float32 [256, 256], replicated, may hold values from -0.3247595 to 0.3247595
- relax: float32 [256], replicated, may hold values from 0.00020833334 to 0.041666668
- pattern: int32 [4, 4], replicated, may hold values 0 or 1
- control_raw: float32 [2, 4, 256, 256], P('ens'), may hold values from -0.22963966 to 0.22963966
- member_drift: float32 [2, 256, 256], P('ens'), may hold values from -0.22963966 to 0.22963966
- amplitude: float32 [4, 96], P(None, 'tm'), may hold values from -0.6 to 0.6
- b1_scale: float32 [2], P('ens'), may hold values from 0.6 to 1.4
- target: float32 [256, 256], replicated, may hold values from -0.375 to 0.375
Outputs:
- gradient: float32 [4, 96], P(None, 'tm')
- fidelity: float32 [1], replicated
All inputs are finite; a program needn't handle non-finite values.
Results may differ from a plain program's by a relative error of at most 0.0003.
Values sent between devices are 32-bit elements; how exact they have to be, the bound alone decides.
No kernel may reach another device: no remote copies, remote signals or barrier semaphores. Data moves between devices by JAX's collectives and lax.ppermute only.
A program may use at most 128 MiB of HBM per device.

v0:
```python
import jax
import jax.numpy as jnp
from jax import lax
from jax.sharding import PartitionSpec as P

ORDER = 6
SQ = 3


def prefix(part, axis, combine, identity, reverse):
    count = lax.axis_size(axis)
    place = lax.axis_index(axis)
    ahead = count - 1 - place if reverse else place
    gathered = lax.all_gather(part, axis)
    state = jnp.zeros_like(part) + jnp.asarray(identity, part.dtype)

    def one(step, state):
        source = count - 1 - step if reverse else step
        return combine(state, lax.dynamic_index_in_dim(gathered, source, 0, False))

    return lax.fori_loop(0, ahead, one, state)


def matmul(first, second):
    return jnp.dot(
        first, second, precision=lax.Precision.HIGHEST, preferred_element_type=jnp.float32
    )


def expand(pattern, states):
    block_size = states // pattern.shape[0]
    return jnp.repeat(jnp.repeat(pattern, block_size, axis=0), block_size, axis=1).astype(
        jnp.float32
    )


def exponent(generator, states):
    unit_matrix = jnp.eye(states, dtype=jnp.float32)
    scaled = generator / 2.0**SQ
    series = unit_matrix + scaled / ORDER
    for degree in range(ORDER - 1, 0, -1):
        series = unit_matrix + matmul(scaled, series) / degree
    for squaring in range(SQ):
        series = matmul(series, series)
    return series


def drift_part(drift_raw, relax, pattern):
    masked = drift_raw * expand(pattern, drift_raw.shape[0])
    return masked - masked.T - jnp.diag(relax)


def forward_join(first_part, second_part):
    return matmul(second_part, first_part)


def backward_join(first_part, second_part):
    return matmul(first_part, second_part)


def per_device(drift_raw, relax, pattern, control_raw, member_drift, amplitude, b1_scale, target):
    states = drift_raw.shape[0]
    unit_matrix = jnp.eye(states, dtype=jnp.float32)
    drift_gen = drift_part(drift_raw, relax, pattern)
    member_control = control_raw[0]
    control_gen = member_control - jnp.swapaxes(member_control, 1, 2)
    offset_raw = member_drift[0]
    member_gen = drift_gen + (offset_raw - offset_raw.T)
    strength = b1_scale[0]

    def one_step(column):
        field = jnp.einsum("c,cab->ab", column, control_gen, precision=lax.Precision.HIGHEST)
        return exponent(member_gen + strength * field, states)

    slice_steps = lax.map(one_step, amplitude.T)

    def forward(running, slice_step):
        updated = matmul(slice_step, running)
        return (updated, updated)

    segment, local_before = lax.scan(forward, unit_matrix, slice_steps)

    def backward(running, slice_step):
        return (matmul(running, slice_step), running)

    unused, local_after = lax.scan(backward, unit_matrix, slice_steps, reverse=True)
    before = prefix(segment, "tm", forward_join, unit_matrix, False)
    after = prefix(segment, "tm", backward_join, unit_matrix, True)
    prefix_all = jnp.einsum("kab,bc->kac", local_before, before, precision=lax.Precision.HIGHEST)
    suffix_all = jnp.einsum("ab,kbc->kac", after, local_after, precision=lax.Precision.HIGHEST)
    left_side = jnp.einsum("kba,bc->kac", suffix_all, target, precision=lax.Precision.HIGHEST)
    projected = jnp.einsum("kab,kcb->kac", left_side, prefix_all, precision=lax.Precision.HIGHEST)
    intersection = jnp.trace(projected[-1])
    gradient_terms = (
        2.0
        * intersection
        * strength
        * jnp.einsum("cab,kab->ck", control_gen, projected, precision=lax.Precision.HIGHEST)
    )
    fidelity_term = intersection * intersection
    total_gradient, total_fidelity = lax.psum((gradient_terms, fidelity_term), "ens")
    return (total_gradient, total_fidelity.reshape(1))


def solution(mesh):
    return jax.shard_map(
        per_device,
        mesh=mesh,
        in_specs=(
            P(),
            P(),
            P(),
            P("ens", None, None, None),
            P("ens", None, None),
            P(None, "tm"),
            P("ens"),
            P(),
        ),
        out_specs=(P(None, "tm"), P()),
        check_vma=False,
    )
```

profile of v0, /device:TPU:0, one launch (start us, length us, event | category | flops | bytes accessed | tf_op | source)
XLA Modules:
  0.0 194.9 jit_solution(6846640040541479574)
XLA Ops:
  8.2 2.5 %copy.11 = f32[1,4,256,256]{2,3,1,0:T(8,128)} copy(f32[1,4,256,256]{3,2,1,0:T(8,128)} %param.21) | data formatting | bytes 2097152 | tf_op args[3]
  10.8 1.4 bitcast_subtract_fusion
  13.2 37.2 %while.62 = (s32[]{:T(128)}, f32[6,256,256]{2,1,0:T(8,128)S(1)}, f32[]{:T(128)}, f32[6,4]{1,0:T(8,128)S(1)}, f32[4,256,256]{2,1,0:T(8,128)S(1)}, /*index=5*/f32[256,256]{1,0:T(8,128)S(1)}, s32[]{:T(128)}) while((s32[]{:T(128)}, f32[6,256,256]{2,1,0:T(8,128)S(1)}, f32[]{:T(128)}, f32[6,4]{1,0:T(8,128)S(1)}, f32[4,256,256]{2,1,0:T(8,128)S(1)}, ...), condition=%wide.region_1.2_spmd, body=%wide.region_0.1_spmd.sunk | while | flops 1615724544 | bytes 7602785 | solution.py:75
  13.2 2.3 %fusion.135 = f32[1,256,256]{2,0,1:T(1,128)S(1)} fusion(f32[4,256,256]{2,1,0:T(8,128)S(1)} %get-tuple-element.488, f32[6,4]{1,0:T(8,128)S(1)} %get-tuple-element.487, s32[]{:T(128)S(6)} %copy.48), kind=kOutput, calls=%fused_computation.11.clone.1 | convolution fusion | flops 3145728 | bytes 1311236 | tf_op jit(solution)/shard_map/while/body/eval_jaxpr/c,cab->ab/dot_general | solution.py:72
  19.4 2.3 %fusion.135 = f32[1,256,256]{2,0,1:T(1,128)S(1)} fusion(f32[4,256,256]{2,1,0:T(8,128)S(1)} %get-tuple-element.488, f32[6,4]{1,0:T(8,128)S(1)} %get-tuple-element.487, s32[]{:T(128)S(6)} %copy.48), kind=kOutput, calls=%fused_computation.11.clone.1 | convolution fusion | flops 3145728 | bytes 1311236 | tf_op jit(solution)/shard_map/while/body/eval_jaxpr/c,cab->ab/dot_general | solution.py:72
  25.6 2.3 %fusion.135 = f32[1,256,256]{2,0,1:T(1,128)S(1)} fusion(f32[4,256,256]{2,1,0:T(8,128)S(1)} %get-tuple-element.488, f32[6,4]{1,0:T(8,128)S(1)} %get-tuple-element.487, s32[]{:T(128)S(6)} %copy.48), kind=kOutput, calls=%fused_computation.11.clone.1 | convolution fusion | flops 3145728 | bytes 1311236 | tf_op jit(solution)/shard_map/while/body/eval_jaxpr/c,cab->ab/dot_general | solution.py:72
  31.8 2.3 %fusion.135 = f32[1,256,256]{2,0,1:T(1,128)S(1)} fusion(f32[4,256,256]{2,1,0:T(8,128)S(1)} %get-tuple-element.488, f32[6,4]{1,0:T(8,128)S(1)} %get-tuple-element.487, s32[]{:T(128)S(6)} %copy.48), kind=kOutput, calls=%fused_computation.11.clone.1 | convolution fusion | flops 3145728 | bytes 1311236 | tf_op jit(solution)/shard_map/while/body/eval_jaxpr/c,cab->ab/dot_general | solution.py:72
  38.1 2.3 %fusion.135 = f32[1,256,256]{2,0,1:T(1,128)S(1)} fusion(f32[4,256,256]{2,1,0:T(8,128)S(1)} %get-tuple-element.488, f32[6,4]{1,0:T(8,128)S(1)} %get-tuple-element.487, s32[]{:T(128)S(6)} %copy.48), kind=kOutput, calls=%fused_computation.11.clone.1 | convolution fusion | flops 3145728 | bytes 1311236 | tf_op jit(solution)/shard_map/while/body/eval_jaxpr/c,cab->ab/dot_general | solution.py:72
  44.3 2.3 %fusion.135 = f32[1,256,256]{2,0,1:T(1,128)S(1)} fusion(f32[4,256,256]{2,1,0:T(8,128)S(1)} %get-tuple-element.488, f32[6,4]{1,0:T(8,128)S(1)} %get-tuple-element.487, s32[]{:T(128)S(6)} %copy.48), kind=kOutput, calls=%fused_computation.11.clone.1 | convolution fusion | flops 3145728 | bytes 1311236 | tf_op jit(solution)/shard_map/while/body/eval_jaxpr/c,cab->ab/dot_general | solution.py:72
  50.5 1.4 broadcast.48
  52.2 12.4 %while.64 = (s32[]{:T(128)}, f32[256,256]{1,0:T(8,128)S(1)}, f32[6,256,256]{2,1,0:T(8,128)}, f32[6,256,256]{2,1,0:T(8,128)}, s32[]{:T(128)}) while((s32[]{:T(128)}, f32[256,256]{1,0:T(8,128)S(1)}, f32[6,256,256]{2,1,0:T(8,128)}, f32[6,256,256]{2,1,0:T(8,128)}, s32[]{:T(128)}) %tuple.129), condition=%wide.region_5.6_spmd, body=%wide.region_4.5_spmd.sunk | while | flops 201326592 | bytes 1573957 | solution.py:81
  52.2 2.1 %bitcast_dynamic-update-slice_fusion.5 = (f32[6,256,256]{2,1,0:T(8,128)}, f32[256,256]{1,0:T(8,128)S(1)}) fusion(f32[6,256,256]{2,1,0:T(8,128)} %get-tuple-element.516, s32[]{:T(128)S(6)} %copy.64, f32[256,256]{1,0:T(8,128)S(1)} %copy.88, f32[6,256,256]{2,1,0:T(8,128)} %get-tuple-element.522), kind=kOutput, calls=%fused_computation.42.clone.1 | convolution fusion | flops 201326592 | bytes 1049600 | tf_op jit(solution)/shard_map/while/body/eval_jaxpr/dot_general | solution.py:25
  54.3 2.0 %bitcast_dynamic-update-slice_fusion.5 = (f32[6,256,256]{2,1,0:T(8,128)}, f32[256,256]{1,0:T(8,128)S(1)}) fusion(f32[6,256,256]{2,1,0:T(8,128)} %get-tuple-element.516, s32[]{:T(128)S(6)} %copy.64, f32[256,256]{1,0:T(8,128)S(1)} %copy.88, f32[6,256,256]{2,1,0:T(8,128)} %get-tuple-element.522), kind=kOutput, calls=%fused_computation.42.clone.1 | convolution fusion | flops 201326592 | bytes 1049600 | tf_op jit(solution)/shard_map/while/body/eval_jaxpr/dot_general | solution.py:25
  56.3 2.1 %bitcast_dynamic-update-slice_fusion.5 = (f32[6,256,256]{2,1,0:T(8,128)}, f32[256,256]{1,0:T(8,128)S(1)}) fusion(f32[6,256,256]{2,1,0:T(8,128)} %get-tuple-element.516, s32[]{:T(128)S(6)} %copy.64, f32[256,256]{1,0:T(8,128)S(1)} %copy.88, f32[6,256,256]{2,1,0:T(8,128)} %get-tuple-element.522), kind=kOutput, calls=%fused_computation.42.clone.1 | convolution fusion | flops 201326592 | bytes 1049600 | tf_op jit(solution)/shard_map/while/body/eval_jaxpr/dot_general | solution.py:25
  58.4 2.0 %bitcast_dynamic-update-slice_fusion.5 = (f32[6,256,256]{2,1,0:T(8,128)}, f32[256,256]{1,0:T(8,128)S(1)}) fusion(f32[6,256,256]{2,1,0:T(8,128)} %get-tuple-element.516, s32[]{:T(128)S(6)} %copy.64, f32[256,256]{1,0:T(8,128)S(1)} %copy.88, f32[6,256,256]{2,1,0:T(8,128)} %get-tuple-element.522), kind=kOutput, calls=%fused_computation.42.clone.1 | convolution fusion | flops 201326592 | bytes 1049600 | tf_op jit(solution)/shard_map/while/body/eval_jaxpr/dot_general | solution.py:25
  60.5 2.0 %bitcast_dynamic-update-slice_fusion.5 = (f32[6,256,256]{2,1,0:T(8,128)}, f32[256,256]{1,0:T(8,128)S(1)}) fusion(f32[6,256,256]{2,1,0:T(8,128)} %get-tuple-element.516, s32[]{:T(128)S(6)} %copy.64, f32[256,256]{1,0:T(8,128)S(1)} %copy.88, f32[6,256,256]{2,1,0:T(8,128)} %get-tuple-element.522), kind=kOutput, calls=%fused_computation.42.clone.1 | convolution fusion | flops 201326592 | bytes 1049600 | tf_op jit(solution)/shard_map/while/body/eval_jaxpr/dot_general | solution.py:25
  62.5 2.1 %bitcast_dynamic-update-slice_fusion.5 = (f32[6,256,256]{2,1,0:T(8,128)}, f32[256,256]{1,0:T(8,128)S(1)}) fusion(f32[6,256,256]{2,1,0:T(8,128)} %get-tuple-element.516, s32[]{:T(128)S(6)} %copy.64, f32[256,256]{1,0:T(8,128)S(1)} %copy.88, f32[6,256,256]{2,1,0:T(8,128)} %get-tuple-element.522), kind=kOutput, calls=%fused_computation.42.clone.1 | convolution fusion | flops 201326592 | bytes 1049600 | tf_op jit(solution)/shard_map/while/body/eval_jaxpr/dot_general | solution.py:25
  66.2 1.3 broadcast.48.clone
  67.5 14.0 %while.63 = (s32[]{:T(128)}, f32[256,256]{0,1:T(8,128)S(1)}, f32[6,256,256]{1,2,0:T(8,128)}, f32[6,256,256]{2,1,0:T(8,128)}, s32[]{:T(128)}, /*index=5*/s32[]{:T(128)}) while((s32[]{:T(128)}, f32[256,256]{0,1:T(8,128)S(1)}, f32[6,256,256]{1,2,0:T(8,128)}, f32[6,256,256]{2,1,0:T(8,128)}, s32[]{:T(128)}, /*index=5*/s32[]{:T(128)}) %tuple.130), condition=%wide.region_3.4_spmd, body=%wide.region_2.3_spmd.sunk | while | flops 201326592 | bytes 1835105 | solution.py:86
  68.2 1.5 convolution_bitcast_fusion.5
  70.6 1.5 convolution_bitcast_fusion.5
  72.9 1.5 convolution_bitcast_fusion.5
  75.2 1.6 convolution_bitcast_fusion.5
  77.6 1.5 convolution_bitcast_fusion.5
  79.9 1.5 convolution_bitcast_fusion.5
  81.5 62.8 %all-gather.3.cloned.1.call-done = f32[4096,256]{1,0:T(8,128)} async-done(((f32[256,256]{1,0:T(8,128)}), f32[4096,256]{1,0:T(8,128)}) %all-gather.3.cloned.1.call-update) | async-done | bytes 4194320 | tf_op jit(solution)/shard_map/all_gather | solution.py:14
  144.3 24.1 %while.65 = (s32[]{:T(128)}, f32[256,256]{0,1:T(8,128)S(1)}, s32[]{:T(128)}, f32[16,256,256]{2,1,0:T(8,128)}, s32[]{:T(128)}, /*index=5*/s32[]{:T(128)}, s32[]{:T(128)}, s32[]{:T(128)}) while((s32[]{:T(128)}, f32[256,256]{0,1:T(8,128)S(1)}, s32[]{:T(128)}, f32[16,256,256]{2,1,0:T(8,128)}, s32[]{:T(128)}, /*index=5*/s32[]{:T(128)}, s32[]{:T(128)}, ...), condition=%wide.region_7.8_spmd, body=%wide.region_6.7_spmd.sunk | while | flops 201326592 | bytes 1310863 | solution.py:21
  144.3 1.5 convolution_bitcast_fusion.6
  145.9 1.5 convolution_bitcast_fusion.6
  147.5 1.5 convolution_bitcast_fusion.6
  149.1 1.5 convolution_bitcast_fusion.6
  150.7 1.5 convolution_bitcast_fusion.6
  152.3 1.5 convolution_bitcast_fusion.6
  154.0 1.5 convolution_bitcast_fusion.6
  155.6 1.5 convolution_bitcast_fusion.6
  157.2 1.5 convolution_bitcast_fusion.6
  158.8 1.5 convolution_bitcast_fusion.6
  160.4 1.5 convolution_bitcast_fusion.6
  162.0 1.5 convolution_bitcast_fusion.6
  163.6 1.5 convolution_bitcast_fusion.6
  165.2 1.5 convolution_bitcast_fusion.6
  166.8 1.5 convolution_bitcast_fusion.6
  168.6 2.8 %fusion.59 = f32[6,256,256]{2,1,0:T(8,128)S(1)} fusion(f32[6,256,256]{1,2,0:T(8,128)} %get-tuple-element.266, f32[256,256]{0,1:T(8,128)S(1)} %get-tuple-element.268), kind=kOutput, calls=%fused_computation.71 | convolution fusion | flops 1207959552 | bytes 3407872 | tf_op jit(solution)/shard_map/ab,kbc->kac/dot_general | solution.py:90
  171.4 1.4 fusion.44
  172.8 1.4 fusion.56
  174.3 1.6 fusion.65
  178.5 5.8 %fusion.49 = f32[4,6]{1,0:T(4,128)S(1)} fusion(f32[6,256,256]{2,1,0:T(8,128)S(1)} %fusion.65, f32[4,256,256]{2,1,0:T(8,128)S(1)} %get-tuple-element.570, f32[]{:T(128)S(6)} %mul.32), kind=kOutput, calls=%fused_computation.60 | convolution fusion | flops 18874392 | bytes 2621540 | tf_op jit(solution)/shard_map/cab,kab->ck/dot_general | solution.py:98
  184.3 3.7 %all-reduce = (f32[4,6]{1,0:T(4,128)}, f32[1]{0:T(128)}) all-reduce(f32[4,6]{1,0:T(4,128)S(1)} %fusion.49, f32[1]{0:T(128)} %bitcast.29), channel_id=1, replica_groups=mesh['tm'=16,'ens'=2] {'ens'}, use_global_device_ids=true, to_apply=%region_11.12 | all-reduce | flops 25 | bytes 200 | tf_op jit(solution)/shard_map/psum | solution.py:101
  (129 shorter events, 31.5 us)
Async XLA Ops:
  7.2 164.2 %copy-start = (f32[256,256]{1,0:T(8,128)S(1)}, f32[256,256]{1,0:T(8,128)}, u32[]{:S(2)}) copy-start(f32[256,256]{1,0:T(8,128)} %param.25) | copy-start | bytes 786436
  7.2 3.6 %copy-start.7 = (f32[1,4,256,256]{3,2,1,0:T(8,128)S(1)}, f32[1,4,256,256]{3,2,1,0:T(8,128)}, u32[]{:S(2)}) copy-start(f32[1,4,256,256]{3,2,1,0:T(8,128)} %param.21) | copy-start | bytes 3145732
  7.2 137.1 %all-gather.3.cloned.1.call-start = ((), (), s32[]{:S(2)}) async-start(), calls=%async_computation | async-start | bytes 4456448 | tf_op jit(solution)/shard_map/all_gather | solution.py:14
  7.3 43.2 %copy-start.1 = (f32[256,256]{1,0:T(8,128)}, f32[256,256]{1,0:T(8,128)S(1)}, u32[]{:S(2)}) copy-start(f32[256,256]{1,0:T(8,128)S(1)} %fusion.62) | copy-start | bytes 786436
  10.8 1.4 copy-start.8
  10.8 1.6 copy-start.9
  10.8 1.7 copy-start.10
  12.2 0.7 copy-start.11
  50.5 1.7 copy-start.5
  50.5 1.7 copy-start.4
  52.2 13.2 %copy-start.2 = (f32[256,256]{1,0:T(8,128)S(1)}, f32[256,256]{1,0:T(8,128)}, u32[]{:S(2)}) copy-start(f32[256,256]{1,0:T(8,128)} %copy-done.1) | copy-start | bytes 786436
  64.6 0.7 copy-start.3
  171.4 1.5 copy-start.6
Sparse Core Ops, SparseCore 0:
  65.5 78.7 all-gather.2
where the time goes:
time: 196 us; the launch traced here: 195 us
  matrix products  90.5 us (46%)
  waiting for transfers between devices  62.9 us (32%)
  between operations  16.9 us (9%)
  local copies, waits for them, and re-layouts  13.1 us (7%)
  other arithmetic  6.3 us (3%)
  blocking collectives  3.68 us (2%)
    dot_general x75, matrix products, matmul(): jnp.dot(first, second, precision=lax.Precision.HIGHEST, preferred_element...  63.3 us
    all_gather x1, waiting for transfers between devices, prefix(): gathered = lax.all_gather(part, axis)  62.8 us
    dot_general x6, matrix products, one_step(): jnp.einsum('c,cab->ab', column, control_gen, precision=lax.Precision.HIGH...  14 us
    dot_general x1, matrix products, per_device(): jnp.einsum('cab,kab->ck', control_gen, projected, precision=lax.Precision...  5.84 us
    unnamed x29, local copies, waits for them, and re-layouts  4.85 us
    dynamic_update_slice x6, local copies, waits for them, and re-layouts, per_device(): slice_steps = lax.map(one_step, amplitude.T)  4.4 us
    add x6, other arithmetic, one_step(): return exponent(member_gen + strength * field, states)  4.09 us
  transfers between devices with their start and end apart: 1, of which 1 were waited for; matrix products, arithmetic and copies ran while one was open for 8% of the time, Pallas kernels for 0%

commit v1 on v0

v1 whole, which is shorter than its diff:
```python
import functools

import jax
import jax.numpy as jnp
from jax import lax
from jax.experimental import pallas as pl
from jax.experimental.pallas import tpu as pltpu
from jax.sharding import PartitionSpec as P

ORDER = 6
SQ = 3
F32 = jnp.float32
BF16 = jnp.bfloat16
VMEM = pl.BlockSpec(memory_space=pltpu.VMEM)
SMEM = pl.BlockSpec(memory_space=pltpu.SMEM)

NN = (((1,), (0,)), ((), ()))
NT = (((1,), (1,)), ((), ()))
TN = (((0,), (0,)), ((), ()))


def parts(value, count):
    out = []
    for _ in range(count):
        part = value.astype(BF16)
        out.append(part)
        value = value - part.astype(F32)
    return out


def dot(first, second, dims=NN):
    return lax.dot_general(first, second, dims, preferred_element_type=F32)


def six(first, second, dims=NN):
    a1, a2, a3 = parts(first, 3)
    b1, b2, b3 = parts(second, 3)
    small = dot(a1, b3, dims) + dot(a2, b2, dims) + dot(a3, b1, dims)
    return dot(a1, b1, dims) + ((dot(a1, b2, dims) + dot(a2, b1, dims)) + small)


def three(first, second, dims=NN):
    a1, a2 = parts(first, 2)
    b1, b2 = parts(second, 2)
    return dot(a1, b1, dims) + (dot(a1, b2, dims) + dot(a2, b1, dims))


def unit(states):
    row = lax.broadcasted_iota(jnp.int32, (states, states), 0)
    column = lax.broadcasted_iota(jnp.int32, (states, states), 1)
    return jnp.where(row == column, 1.0, 0.0).astype(F32)


def exponents(scaled):
    second = [six(x, x) for x in scaled]
    third = [six(x, y) for x, y in zip(scaled, second)]
    rest = [
        x + y * 0.5 + z * (1.0 / 6) + three(z, x * (1.0 / 24) + y * (1.0 / 120) + z * (1.0 / 720))
        for x, y, z in zip(scaled, second, third)
    ]
    for _ in range(SQ):
        rest = [2.0 * q + six(q, q) for q in rest]
    return rest


def step_kernel(
    amplitude, strength, mask, relax, drift_raw, member_drift, control_raw,
    control_out, step_out, pair_out, before_out, segment_out,
):
    states = drift_raw.shape[0]
    count = step_out.shape[0]
    fields = control_raw.shape[0]
    row = lax.broadcasted_iota(jnp.int32, (states, states), 0)
    column = lax.broadcasted_iota(jnp.int32, (states, states), 1)
    coupled = drift_raw[...] * mask[...] + member_drift[...]
    base = coupled - coupled.T - jnp.where(row == column, relax[...], 0.0)
    for c in range(fields):
        control_out[c] = control_raw[c] - control_raw[c].T
    scaled = []
    for k in range(count):
        field = amplitude[0, k] * control_out[0]
        for c in range(1, fields):
            field = field + amplitude[c, k] * control_out[c]
        scaled.append((base + strength[0] * field) * (1.0 / 2.0**SQ))
    eye = jnp.where(row == column, 1.0, 0.0).astype(F32)
    steps = [eye + q for q in exponents(scaled)]
    for k in range(count):
        step_out[k] = steps[k]
    pairs = []
    for j in range(pair_out.shape[0]):
        pairs.append(six(steps[2 * j + 1], steps[2 * j]) if 2 * j + 1 < count else steps[2 * j])
        pair_out[j] = pairs[j]
    running = pairs[0]
    for j in range(1, len(pairs)):
        before_out[j - 1] = running
        running = six(pairs[j], running)
    segment_out[...] = running


def local_kernel(step, pair, before, segment, prefix_out, suffix_out):
    count = step.shape[0]
    halves = pair.shape[0]
    eye = unit(step.shape[1])
    prefix_out[0] = step[0]
    prefix_out[count - 1] = segment[...]
    for j in range(halves):
        if j > 0:
            if 2 * j < count - 1:
                prefix_out[2 * j] = six(step[2 * j], before[j - 1])
        if 2 * j + 1 < count - 1:
            prefix_out[2 * j + 1] = before[j]
    running = None
    for j in reversed(range(halves)):
        if 2 * j + 1 < count:
            suffix_out[2 * j + 1] = eye if running is None else running
            suffix_out[2 * j] = step[2 * j + 1] if running is None else six(running, step[2 * j + 1])
        else:
            suffix_out[2 * j] = eye
        running = pair[j] if running is None else (six(running, pair[j]) if j > 0 else running)


def join_kernel(bit, held, other, joined):
    upper = bit[0] == 1
    mine, theirs = held[...], other[...]
    joined[...] = six(jnp.where(upper, mine, theirs), jnp.where(upper, theirs, mine))


def first_reach_kernel(bit, other, after_out, before_out):
    upper = bit[0] == 1
    eye = unit(other.shape[0])
    after_out[...] = jnp.where(upper, eye, other[...])
    before_out[...] = jnp.where(upper, other[...], eye)


def reach_kernel(bit, other, after, before, after_out, before_out):
    upper = bit[0] == 1
    product = six(jnp.where(upper, before[...], other[...]), jnp.where(upper, other[...], after[...]))
    after_out[...] = jnp.where(upper, after[...], product)
    before_out[...] = jnp.where(upper, product, before[...])


def sides_kernel(bit, target, after, before, suffix, prefix, left_out, right_out, left, right):
    count = prefix.shape[0]

    @pl.when(bit[0] == 1)
    def _():
        left[...] = three(after[...], target[...], TN)
        right[...] = before[...].T

    @pl.when(bit[0] == 0)
    def _():
        left[...] = after[...].T
        right[...] = three(target[...], before[...], NT)

    for k in range(count):
        left_out[k] = three(suffix[k], left[...], TN) if k < count - 1 else left[...]
        right_out[k] = three(right[...], prefix[k], NT)


def gradient_kernel(strength, other, left, right, control, out):
    count, states = left.shape[0], left.shape[1]
    fields = control.shape[0]
    middle = three(left[...].reshape(count * states, states), other[...], NT)
    lane = lax.broadcasted_iota(jnp.int32, out.shape, 1)
    line = lax.broadcasted_iota(jnp.int32, out.shape, 0)
    row = lax.broadcasted_iota(jnp.int32, (states, states), 0)
    column = lax.broadcasted_iota(jnp.int32, (states, states), 1)
    total = jnp.zeros(out.shape, F32)
    overlap = None
    for k in range(count):
        projected = three(middle[k * states : (k + 1) * states], right[k])
        if k == count - 1:
            overlap = jnp.sum(jnp.where(row == column, projected, 0.0))
        for c in range(fields):
            term = jnp.sum(control[c] * projected)
            total = jnp.where((line == c) & (lane == k), term, total)
    total = total * (2.0 * overlap * strength[0])
    out[...] = jnp.where((line == 0) & (lane == count), overlap * overlap, total)


def call(kernel, shapes, in_specs, name, flops=0, scratch=()):
    many = isinstance(shapes, list)
    made = [jax.ShapeDtypeStruct(s, F32) for s in (shapes if many else [shapes])]
    return pl.pallas_call(
        kernel,
        out_shape=made if many else made[0],
        in_specs=in_specs,
        out_specs=[VMEM] * len(made) if many else VMEM,
        scratch_shapes=list(scratch),
        compiler_params=pltpu.CompilerParams(vmem_limit_bytes=48 * 2**20),
        cost_estimate=pl.CostEstimate(flops=flops, bytes_accessed=2**20, transcendentals=0),
        name=name,
    )


def per_device(
    drift_raw, relax, pattern, control_raw, member_drift, amplitude, b1_scale, target, *, segments, members
):
    states = drift_raw.shape[0]
    count = amplitude.shape[1]
    halves = (count + 1) // 2
    fields = control_raw.shape[1]
    square = (states, states)
    product = 12 * states**3
    block = states // pattern.shape[0]
    mask = jnp.repeat(jnp.repeat(pattern, block, axis=0), block, axis=1).astype(F32)
    bits = segments.bit_length() - 1
    turn = bits // 2 if members == 2 else 0

    def turned(place, member):
        shift = turn if member % 2 else 0
        return ((place >> shift) | (place << (bits - shift))) & (segments - 1)

    def flat(place, member):
        return place * members + member

    both = ("tm", "ens")
    place = lax.axis_index("tm")
    member = lax.axis_index("ens")
    segment = jnp.where(member % 2 == 1, turned(place, 1), place)
    digits = [((segment >> r) & 1).astype(jnp.int32).reshape(1) for r in range(bits)]

    if turn:
        amplitude = lax.ppermute(
            amplitude,
            both,
            [(flat(turned(p, e), e), flat(p, e)) for p in range(segments) for e in range(members)],
        )
    control, step, pair, local, held = call(
        step_kernel,
        [(fields,) + square, (count,) + square, (halves,) + square, (max(halves - 1, 1),) + square, square],
        [SMEM, SMEM] + [VMEM] * 5,
        "steps",
        flops=50 * product,
    )(amplitude, b1_scale, mask, relax.reshape(1, states), drift_raw, member_drift[0], control_raw[0])

    after = before = prefix = suffix = None
    for r in range(bits):
        pairs = []
        for e in range(members):
            shift = turn if e % 2 else 0
            flip = 1 << ((r + shift) % bits)
            pairs += [(flat(p, e), flat(p ^ flip, e)) for p in range(segments)]
        other = lax.ppermute(held, both, pairs)
        if r == 0:
            prefix, suffix = call(
                local_kernel, [(count,) + square] * 2, [VMEM] * 4, "local", flops=5 * product
            )(step, pair, local, held)
        if r < bits - 1:
            held = call(join_kernel, square, [SMEM, VMEM, VMEM], "join", flops=product)(digits[r], held, other)
            if after is None:
                after, before = call(
                    first_reach_kernel, [square] * 2, [SMEM, VMEM], "reach_first", flops=product // 4
                )(digits[r], other)
            else:
                after, before = call(
                    reach_kernel, [square] * 2, [SMEM] + [VMEM] * 3, "reach", flops=product
                )(digits[r], other, after, before)
    left, right = call(
        sides_kernel,
        [(count,) + square] * 2,
        [SMEM] + [VMEM] * 5,
        "sides",
        flops=6 * product,
        scratch=[pltpu.VMEM(square, F32)] * 2,
    )(digits[-1], target, after, before, suffix, prefix)
    mine = call(gradient_kernel, (8, 128), [SMEM] + [VMEM] * 4, "gradient", flops=6 * product)(
        b1_scale, other, left, right, control
    )
    if turn:
        first = [(flat(p, 1), flat(turned(p, 1), 0)) for p in range(segments)]
        first += [(flat(p, 0), flat(p, 1)) for p in range(segments)]
        second = [(flat(p, 1), flat(turned(p, 1), 1)) for p in range(segments)]
        second += [(flat(p, 0), flat(p, 0)) for p in range(segments)]
        total = lax.ppermute(mine, both, first) + lax.ppermute(mine, both, second)
    else:
        total = lax.psum(mine, "ens")
    return (total[:fields, :count], total[0, count : count + 1])


def solution(mesh):
    return jax.shard_map(
        functools.partial(per_device, segments=mesh.shape["tm"], members=mesh.shape["ens"]),
        mesh=mesh,
        in_specs=(
            P(),
            P(),
            P(),
            P("ens", None, None, None),
            P("ens", None, None),
            P(None, "tm"),
            P("ens"),
            P(),
        ),
        out_specs=(P(None, "tm"), P()),
        check_vma=False,
    )
```

time: 196 us -> 67.6 us (0.34)
  the two profiles are of different devices: /device:TPU:0 before, /device:TPU:7 now
where the time goes in v1:
time: 67.6 us; the launch traced here: 67.1 us
  waiting for transfers between devices  23.1 us (34%)
  Pallas kernels  21.5 us (32%)
  starting transfers between devices  10.6 us (16%)
  local copies, waits for them, and re-layouts  9.7 us (14%)
  between operations  1.47 us (2%)
  other arithmetic  0.69 us (1%)
    ppermute x4, waiting for transfers between devices, per_device(): other = lax.ppermute(held, both, pairs)  19.2 us
    pallas_call x1, Pallas kernels, per_device(): call(step_kernel, [(fields,) + square, (count,) + square, (halves,) + squ...  10.6 us
    unnamed x18, local copies, waits for them, and re-layouts  8.13 us
    ppermute x2, starting transfers between devices, per_device(): total = lax.ppermute(mine, both, first) + lax.ppermute(mine, both, second)  5.19 us
    ppermute x1, starting transfers between devices, per_device(): lax.ppermute(amplitude, both, [(flat(turned(p, e), e), flat(p, e)) for p...  5.14 us
    pallas_call x1, Pallas kernels, per_device(): call(local_kernel, [(count,) + square] * 2, [VMEM] * 4, 'local', flops=5...  3.16 us
    pallas_call x1, Pallas kernels, per_device(): call(sides_kernel, [(count,) + square] * 2, [SMEM] + [VMEM] * 5, 'sides',...  3.1 us
    ppermute x2, waiting for transfers between devices, per_device(): total = lax.ppermute(mine, both, first) + lax.ppermute(mine, both, second)  2.74 us
  transfers between devices with their start and end apart: 7, of which 5 were waited for; matrix products, arithmetic and copies ran while one was open for 2% of the time, Pallas kernels for 11%

profile of v1, /device:TPU:7, one launch (start us, length us, event | category | flops | bytes accessed | tf_op | source)
XLA Modules:
  0.0 67.1 jit_solution(13527441441744411545)
XLA Ops:
  0.6 5.1 %collective-permute-start = (f32[4,6]{1,0:T(4,128)}, f32[4,6]{1,0:T(4,128)S(1)}, u32[]{:S(2)}, u32[]{:S(2)}) collective-permute-start(f32[4,6]{1,0:T(4,128)} %param.13), channel_id=1, source_target_pairs={{0,0},{1,1},{2,2},{9,3},{4,4},{17,5},{6,6},{25,7},{8,8},{3,9},{10,... | collective-permute-start | bytes 296 | tf_op jit(solution)/shard_map/ppermute | solution.py:224
  6.4 0.7 %convert_element_type.7 = f32[4,4]{1,0:T(4,128)S(1)} convert(s32[4,4]{1,0:T(4,128)} %param.10) | non-fusion elementwise | flops 16 | bytes 128 | tf_op jit(solution)/shard_map/convert_element_type | solution.py:206
  7.1 0.1 copy.10
  7.2 0.1 broadcast_in_dim.6
  7.3 0.1 convert_element_type.8
  7.4 0.1 copy.11.mask
  7.5 1.2 %collective-permute-done.amplitude = f32[4,6]{1,0:T(4,128)S(1)} collective-permute-done((f32[4,6]{1,0:T(4,128)}, f32[4,6]{1,0:T(4,128)S(1)}, u32[]{:S(2)}, u32[]{:S(2)}) %collective-permute-start) | collective-permute-done | bytes 128 | tf_op jit(solution)/shard_map/ppermute | solution.py:224
  8.8 0.0 copy-start
  8.8 1.2 %copy-done = f32[1,4,256,256]{3,2,1,0:T(8,128)S(1)} copy-done((f32[1,4,256,256]{3,2,1,0:T(8,128)S(1)}, f32[1,4,256,256]{3,2,1,0:T(8,128)}, u32[]{:S(2)}) %copy-start) | copy-done | bytes 1048600
  10.0 0.0 copy-start.1
  10.0 0.9 %copy-done.1 = f32[256,256]{1,0:T(8,128)S(1)} copy-done((f32[256,256]{1,0:T(8,128)S(1)}, f32[256,256]{1,0:T(8,128)}, u32[]{:S(2)}) %copy-start.1) | copy-done | bytes 262168
  10.9 0.0 copy-start.2
  10.9 0.9 %copy-done.2 = f32[1,256,256]{2,1,0:T(8,128)S(1)} copy-done((f32[1,256,256]{2,1,0:T(8,128)S(1)}, f32[1,256,256]{2,1,0:T(8,128)}, u32[]{:S(2)}) %copy-start.2) | copy-done | bytes 262168
  11.9 0.0 copy-start.4
  11.9 0.7 %copy-done.4 = f32[256]{0:T(256)S(1)} copy-done((f32[256]{0:T(256)S(1)}, f32[256]{0:T(256)}, u32[]{:S(2)}) %copy-start.4) | copy-done | bytes 1048
  12.6 10.6 %steps.1 = (f32[4,256,256]{2,1,0:T(8,128)S(1)}, f32[6,256,256]{2,1,0:T(8,128)S(1)}, f32[3,256,256]{2,1,0:T(8,128)S(1)}, f32[2,256,256]{2,1,0:T(8,128)S(1)}, f32[256,256]{1,0:T(8,128)S(1)}) custom-call(f32[4,6]{1,0:T(4,128)S(1)} %collective-permute-done.amplitude, f32[1]{0:T(128)S(6)} %copy.12.strength, f32[256,256]{1,0:T(8,128)S(1)} %copy.11.mask, ...), custom_call_target="tpu_custom_call" | custom-call | flops 10066329600 | bytes 1048576 | tf_op jit(solution)/shard_map/steps/pallas_call | solution.py:229
  23.1 0.0 copy-start.6
  23.1 1.2 %copy-done.6 = f32[6,256,256]{2,1,0:T(8,128)} copy-done((f32[6,256,256]{2,1,0:T(8,128)}, f32[6,256,256]{2,1,0:T(8,128)S(1)}, u32[]{:S(2)}) %copy-start.6) | copy-done | bytes 1572888
  24.3 0.0 copy-start.7
  24.3 0.9 %copy-done.7 = f32[3,256,256]{2,1,0:T(8,128)} copy-done((f32[3,256,256]{2,1,0:T(8,128)}, f32[3,256,256]{2,1,0:T(8,128)S(1)}, u32[]{:S(2)}) %copy-start.7) | copy-done | bytes 786456
  25.2 0.0 collective-permute-start.1
  25.2 5.2 %collective-permute-done.1.other = f32[256,256]{1,0:T(8,128)S(1)} collective-permute-done((f32[256,256]{1,0:T(8,128)S(1)}, f32[256,256]{1,0:T(8,128)S(1)}, u32[]{:S(2)}, u32[]{:S(2)}) %collective-permute-start.1) | collective-permute-done | bytes 262176 | tf_op jit(solution)/shard_map/ppermute | solution.py:244
  30.4 0.4 join.3.held
  30.8 0.1 collective-permute-start.2
  30.9 8.7 %collective-permute-done.2.other = f32[256,256]{1,0:T(8,128)S(1)} collective-permute-done((f32[256,256]{1,0:T(8,128)S(1)}, f32[256,256]{1,0:T(8,128)S(1)}, u32[]{:S(2)}, u32[]{:S(2)}) %collective-permute-start.2) | collective-permute-done | bytes 262176 | tf_op jit(solution)/shard_map/ppermute | solution.py:244
  39.6 0.4 join.4.held
  40.0 0.1 collective-permute-start.3
  40.1 5.2 %collective-permute-done.3.other = f32[256,256]{1,0:T(8,128)S(1)} collective-permute-done((f32[256,256]{1,0:T(8,128)S(1)}, f32[256,256]{1,0:T(8,128)S(1)}, u32[]{:S(2)}, u32[]{:S(2)}) %collective-permute-start.3) | collective-permute-done | bytes 262176 | tf_op jit(solution)/shard_map/ppermute | solution.py:244
  45.3 0.4 join.5
  45.7 0.1 collective-permute-start.4
  45.8 0.0 copy-start.8
  45.8 1.1 %copy-done.8 = f32[3,256,256]{2,1,0:T(8,128)S(1)} copy-done((f32[3,256,256]{2,1,0:T(8,128)S(1)}, f32[3,256,256]{2,1,0:T(8,128)}, u32[]{:S(2)}) %copy-start.8) | copy-done | bytes 786456
  46.9 3.2 %local.1 = (f32[6,256,256]{2,1,0:T(8,128)S(1)}, f32[6,256,256]{2,1,0:T(8,128)S(1)}) custom-call(f32[6,256,256]{2,1,0:T(8,128)} %copy-done.6, f32[3,256,256]{2,1,0:T(8,128)S(1)} %copy-done.8, f32[2,256,256]{2,1,0:T(8,128)S(1)} %get-tuple-element.26.before, f32[256,256]{1,0:T(8,128)S(1)} %get-tuple-element.17.held.segment), custom_call_target="tpu_custom_call" | custom-call | flops 1006632960 | bytes 1048576 | tf_op jit(solution)/shard_map/local/pallas_call | solution.py:246
  50.1 0.0 copy-start.5
  50.1 1.2 %copy-done.5 = f32[6,256,256]{2,1,0:T(8,128)} copy-done((f32[6,256,256]{2,1,0:T(8,128)}, f32[6,256,256]{2,1,0:T(8,128)S(1)}, u32[]{:S(2)}) %copy-start.5) | copy-done | bytes 1572888
  51.2 0.0 copy-start.3
  51.3 0.4 reach.2
  51.7 0.6 reach.3
  52.3 0.0 copy-done.3
  52.3 3.1 %sides.1 = (f32[6,256,256]{2,1,0:T(8,128)S(1)}, f32[6,256,256]{2,1,0:T(8,128)S(1)}) custom-call(s32[1]{0:T(128)} %bitcast.7.bit, f32[256,256]{1,0:T(8,128)S(1)} %copy-done.3, f32[256,256]{1,0:T(8,128)S(1)} %get-tuple-element.22.after, f32[256,256]{1,0:T(8,128)S(1)} %get-tuple-element.23.before, f32[6,256,256]{2,1,0:T(8,128)S(1)} %get-tuple-element.27.suffix, ...), custom_call_target="tpu_custom_call" | custom-call | flops 1207959552 | bytes 1048576 | tf_op jit(solution)/shard_map/sides/pallas_call | solution.py:259
  55.4 0.0 collective-permute-done.4.other
  55.4 2.5 %gradient.1 = f32[8,128]{1,0:T(8,128)S(1)} custom-call(f32[1]{0:T(128)S(6)} %copy.12.strength, f32[256,256]{1,0:T(8,128)S(1)} %collective-permute-done.4.other, f32[6,256,256]{2,1,0:T(8,128)S(1)} %get-tuple-element.29.left, f32[6,256,256]{2,1,0:T(8,128)S(1)} %get-tuple-element.30.right, f32[4,256,256]{2,1,0:T(8,128)S(1)} %get-tuple-element.31.control), custom_call_target="tpu_custom_call" | custom-call | flops 1207959552 | bytes 1048576 | tf_op jit(solution)/shard_map/gradient/pallas_call | solution.py:267
  58.0 5.1 %collective-permute-start.6 = (f32[8,128]{1,0:T(8,128)S(1)}, f32[8,128]{1,0:T(8,128)S(1)}, u32[]{:S(2)}, u32[]{:S(2)}) collective-permute-start(f32[8,128]{1,0:T(8,128)S(1)} %gradient.1), channel_id=1, source_target_pairs={{1,1},{3,9},{5,17},{7,25},{9,3},{11,11},{13,19},{15,27},{17,5},{19... | collective-permute-start | bytes 12296 | tf_op jit(solution)/shard_map/ppermute | solution.py:275
  63.1 0.1 collective-permute-start.5
  63.2 2.7 %collective-permute-done.6 = f32[8,128]{1,0:T(8,128)S(1)} collective-permute-done((f32[8,128]{1,0:T(8,128)S(1)}, f32[8,128]{1,0:T(8,128)S(1)}, u32[]{:S(2)}, u32[]{:S(2)}) %collective-permute-start.6) | collective-permute-done | bytes 4128 | tf_op jit(solution)/shard_map/ppermute | solution.py:275
  65.9 0.0 collective-permute-done.5
  65.9 0.6 slice.7
  66.5 0.6 slice.6
  (3 shorter events, 0.1 us)
Async XLA Ops:
  0.6 8.1 %collective-permute-start = (f32[4,6]{1,0:T(4,128)}, f32[4,6]{1,0:T(4,128)S(1)}, u32[]{:S(2)}, u32[]{:S(2)}) collective-permute-start(f32[4,6]{1,0:T(4,128)} %param.13), channel_id=1, source_target_pairs={{0,0},{1,1},{2,2},{9,3},{4,4},{17,5},{6,6},{25,7},{8,8},{3,9},{10,... | collective-permute-start | bytes 296 | tf_op jit(solution)/shard_map/ppermute | solution.py:224
  8.8 1.2 %copy-start = (f32[1,4,256,256]{3,2,1,0:T(8,128)S(1)}, f32[1,4,256,256]{3,2,1,0:T(8,128)}, u32[]{:S(2)}) copy-start(f32[1,4,256,256]{3,2,1,0:T(8,128)} %param.11) | copy-start | bytes 3145732
  10.0 0.9 %copy-start.1 = (f32[256,256]{1,0:T(8,128)S(1)}, f32[256,256]{1,0:T(8,128)}, u32[]{:S(2)}) copy-start(f32[256,256]{1,0:T(8,128)} %drift_raw.1) | copy-start | bytes 786436
  10.9 0.9 %copy-start.2 = (f32[1,256,256]{2,1,0:T(8,128)S(1)}, f32[1,256,256]{2,1,0:T(8,128)}, u32[]{:S(2)}) copy-start(f32[1,256,256]{2,1,0:T(8,128)} %param.12) | copy-start | bytes 786436
  11.9 0.7 %copy-start.4 = (f32[256]{0:T(256)S(1)}, f32[256]{0:T(256)}, u32[]{:S(2)}) copy-start(f32[256]{0:T(256)} %param.9) | copy-start | bytes 3076
  23.1 1.2 %copy-start.6 = (f32[6,256,256]{2,1,0:T(8,128)}, f32[6,256,256]{2,1,0:T(8,128)S(1)}, u32[]{:S(2)}) copy-start(f32[6,256,256]{2,1,0:T(8,128)S(1)} %get-tuple-element.24.step) | copy-start | bytes 4718596
  24.3 0.9 %copy-start.7 = (f32[3,256,256]{2,1,0:T(8,128)}, f32[3,256,256]{2,1,0:T(8,128)S(1)}, u32[]{:S(2)}) copy-start(f32[3,256,256]{2,1,0:T(8,128)S(1)} %get-tuple-element.25.pair) | copy-start | bytes 2359300
  25.2 5.2 %collective-permute-start.1 = (f32[256,256]{1,0:T(8,128)S(1)}, f32[256,256]{1,0:T(8,128)S(1)}, u32[]{:S(2)}, u32[]{:S(2)}) collective-permute-start(f32[256,256]{1,0:T(8,128)S(1)} %get-tuple-element.17.held.segment), channel_id=1, source_target_pairs={{0,2},{2,0},{4,6},{6,4},{8,10},{10,8},{12,14},{14,12},{16,18},{18,... | collective-permute-start | bytes 786440 | tf_op jit(solution)/shard_map/ppermute | solution.py:244
  30.8 8.8 %collective-permute-start.2 = (f32[256,256]{1,0:T(8,128)S(1)}, f32[256,256]{1,0:T(8,128)S(1)}, u32[]{:S(2)}, u32[]{:S(2)}) collective-permute-start(f32[256,256]{1,0:T(8,128)S(1)} %join.3.held), channel_id=1, source_target_pairs={{0,4},{2,6},{4,0},{6,2},{8,12},{10,14},{12,8},{14,10},{16,20},{18,... | collective-permute-start | bytes 786440 | tf_op jit(solution)/shard_map/ppermute | solution.py:244
  40.0 5.3 %collective-permute-start.3 = (f32[256,256]{1,0:T(8,128)S(1)}, f32[256,256]{1,0:T(8,128)S(1)}, u32[]{:S(2)}, u32[]{:S(2)}) collective-permute-start(f32[256,256]{1,0:T(8,128)S(1)} %join.4.held), channel_id=1, source_target_pairs={{0,8},{2,10},{4,12},{6,14},{8,0},{10,2},{12,4},{14,6},{16,24},{18,... | collective-permute-start | bytes 786440 | tf_op jit(solution)/shard_map/ppermute | solution.py:244
  45.7 9.7 %collective-permute-start.4 = (f32[256,256]{1,0:T(8,128)S(1)}, f32[256,256]{1,0:T(8,128)S(1)}, u32[]{:S(2)}, u32[]{:S(2)}) collective-permute-start(f32[256,256]{1,0:T(8,128)S(1)} %join.5), channel_id=1, source_target_pairs={{0,16},{2,18},{4,20},{6,22},{8,24},{10,26},{12,28},{14,30},{16,0},... | collective-permute-start | bytes 786440 | tf_op jit(solution)/shard_map/ppermute | solution.py:244
  45.8 1.1 %copy-start.8 = (f32[3,256,256]{2,1,0:T(8,128)S(1)}, f32[3,256,256]{2,1,0:T(8,128)}, u32[]{:S(2)}) copy-start(f32[3,256,256]{2,1,0:T(8,128)} %copy-done.7) | copy-start | bytes 2359300
  50.1 1.2 %copy-start.5 = (f32[6,256,256]{2,1,0:T(8,128)}, f32[6,256,256]{2,1,0:T(8,128)S(1)}, u32[]{:S(2)}) copy-start(f32[6,256,256]{2,1,0:T(8,128)S(1)} %get-tuple-element.28.prefix) | copy-start | bytes 4718596
  51.2 1.1 %copy-start.3 = (f32[256,256]{1,0:T(8,128)S(1)}, f32[256,256]{1,0:T(8,128)}, u32[]{:S(2)}) copy-start(f32[256,256]{1,0:T(8,128)} %target.1) | copy-start | bytes 786436
  58.0 7.9 %collective-permute-start.6 = (f32[8,128]{1,0:T(8,128)S(1)}, f32[8,128]{1,0:T(8,128)S(1)}, u32[]{:S(2)}, u32[]{:S(2)}) collective-permute-start(f32[8,128]{1,0:T(8,128)S(1)} %gradient.1), channel_id=1, source_target_pairs={{1,1},{3,9},{5,17},{7,25},{9,3},{11,11},{13,19},{15,27},{17,5},{19... | collective-permute-start | bytes 12296 | tf_op jit(solution)/shard_map/ppermute | solution.py:275
  63.1 2.8 %collective-permute-start.5 = (f32[8,128]{1,0:T(8,128)S(1)}, f32[8,128]{1,0:T(8,128)S(1)}, u32[]{:S(2)}, u32[]{:S(2)}) collective-permute-start(f32[8,128]{1,0:T(8,128)S(1)} %gradient.1), channel_id=1, source_target_pairs={{1,0},{3,8},{5,16},{7,24},{9,2},{11,10},{13,18},{15,26},{17,4},{19... | collective-permute-start | bytes 12296 | tf_op jit(solution)/shard_map/ppermute | solution.py:275

commit v2 on v1

--- a/solution.py
+++ b/solution.py
@@ -13,6 +13,7 @@
 BF16 = jnp.bfloat16
 VMEM = pl.BlockSpec(memory_space=pltpu.VMEM)
 SMEM = pl.BlockSpec(memory_space=pltpu.SMEM)
+HBM = pl.BlockSpec(memory_space=pltpu.HBM)
 
 NN = (((1,), (0,)), ((), ()))
 NT = (((1,), (1,)), ((), ()))
@@ -63,26 +64,51 @@
     return rest
 
 
-def step_kernel(
-    amplitude, strength, mask, relax, drift_raw, member_drift, control_raw,
-    control_out, step_out, pair_out, before_out, segment_out,
+def generator_kernel(
+    strength, pattern, relax, drift_raw, member_drift, control_raw, base_out, control_out,
+    relax_in, drift_in, member_in, control_in, coupled, arrived,
 ):
-    states = drift_raw.shape[0]
-    count = step_out.shape[0]
-    fields = control_raw.shape[0]
+    fields, states = control_raw.shape[0], control_raw.shape[1]
+    moves = [
+        pltpu.make_async_copy(drift_raw, drift_in, arrived.at[0]),
+        pltpu.make_async_copy(member_drift, member_in, arrived.at[1]),
+        pltpu.make_async_copy(relax, relax_in, arrived.at[2]),
+    ]
+    moves += [
+        pltpu.make_async_copy(control_raw.at[c], control_in.at[c], arrived.at[3 + c]) for c in range(fields)
+    ]
+    for move in moves:
+        move.start()
+    blocks = pattern.shape[0]
+    size = states // blocks
+    part = lax.broadcasted_iota(jnp.int32, (1, states), 1) // size
+    for move in moves[:3]:
+        move.wait()
+    for i in range(blocks):
+        line = jnp.zeros((1, states), F32)
+        for j in range(blocks):
+            line = jnp.where(part == j, pattern[i, j].astype(F32), line)
+        rows = slice(i * size, (i + 1) * size)
+        coupled[rows] = drift_in[rows] * line + member_in[rows]
     row = lax.broadcasted_iota(jnp.int32, (states, states), 0)
     column = lax.broadcasted_iota(jnp.int32, (states, states), 1)
-    coupled = drift_raw[...] * mask[...] + member_drift[...]
-    base = coupled - coupled.T - jnp.where(row == column, relax[...], 0.0)
+    base_out[...] = coupled[...] - coupled[...].T - jnp.where(row == column, relax_in[...], 0.0)
     for c in range(fields):
-        control_out[c] = control_raw[c] - control_raw[c].T
+        moves[3 + c].wait()
+        control_out[c] = strength[0] * (control_in[c] - control_in[c].T)
+
+
+def step_kernel(amplitude, base, control, step_out, pair_out, before_out, segment_out):
+    states = base.shape[0]
+    count = step_out.shape[0]
+    fields = control.shape[0]
     scaled = []
     for k in range(count):
-        field = amplitude[0, k] * control_out[0]
+        field = amplitude[0, k] * control[0]
         for c in range(1, fields):
-            field = field + amplitude[c, k] * control_out[c]
-        scaled.append((base + strength[0] * field) * (1.0 / 2.0**SQ))
-    eye = jnp.where(row == column, 1.0, 0.0).astype(F32)
+            field = field + amplitude[c, k] * control[c]
+        scaled.append((base[...] + field) * (1.0 / 2.0**SQ))
+    eye = unit(states)
     steps = [eye + q for q in exponents(scaled)]
     for k in range(count):
         step_out[k] = steps[k]
@@ -119,35 +145,36 @@
         running = pair[j] if running is None else (six(running, pair[j]) if j > 0 else running)
 
 
-def join_kernel(bit, held, other, joined):
-    upper = bit[0] == 1
+def join_kernel(place, held, other, joined):
+    upper = place() == 1
     mine, theirs = held[...], other[...]
     joined[...] = six(jnp.where(upper, mine, theirs), jnp.where(upper, theirs, mine))
 
 
-def first_reach_kernel(bit, other, after_out, before_out):
-    upper = bit[0] == 1
+def first_reach_kernel(place, other, after_out, before_out):
+    upper = place() == 1
     eye = unit(other.shape[0])
     after_out[...] = jnp.where(upper, eye, other[...])
     before_out[...] = jnp.where(upper, other[...], eye)
 
 
-def reach_kernel(bit, other, after, before, after_out, before_out):
-    upper = bit[0] == 1
+def reach_kernel(place, other, after, before, after_out, before_out):
+    upper = place() == 1
     product = six(jnp.where(upper, before[...], other[...]), jnp.where(upper, other[...], after[...]))
     after_out[...] = jnp.where(upper, after[...], product)
     before_out[...] = jnp.where(upper, product, before[...])
 
 
-def sides_kernel(bit, target, after, before, suffix, prefix, left_out, right_out, left, right):
+def sides_kernel(place, target, after, before, suffix, prefix, left_out, right_out, left, right):
     count = prefix.shape[0]
-
-    @pl.when(bit[0] == 1)
+    bit = place()
+
+    @pl.when(bit == 1)
     def _():
         left[...] = three(after[...], target[...], TN)
         right[...] = before[...].T
 
-    @pl.when(bit[0] == 0)
+    @pl.when(bit == 0)
     def _():
         left[...] = after[...].T
         right[...] = three(target[...], before[...], NT)
@@ -157,7 +184,7 @@
         right_out[k] = three(right[...], prefix[k], NT)
 
 
-def gradient_kernel(strength, other, left, right, control, out):
+def gradient_kernel(other, left, right, control, out):
     count, states = left.shape[0], left.shape[1]
     fields = control.shape[0]
     middle = three(left[...].reshape(count * states, states), other[...], NT)
@@ -174,20 +201,27 @@
         for c in range(fields):
             term = jnp.sum(control[c] * projected)
             total = jnp.where((line == c) & (lane == k), term, total)
-    total = total * (2.0 * overlap * strength[0])
+    total = total * (2.0 * overlap)
     out[...] = jnp.where((line == 0) & (lane == count), overlap * overlap, total)
 
 
-def call(kernel, shapes, in_specs, name, flops=0, scratch=()):
+def finish_kernel(first, second, gradient_out, fidelity_out):
+    fields, count = gradient_out.shape
+    total = first[...] + second[...]
+    gradient_out[...] = total[:fields, :count]
+    fidelity_out[...] = total[:1, count : count + 1]
+
+
+def call(kernel, shapes, in_specs, name, flops=0, scratch=(), room=12):
     many = isinstance(shapes, list)
-    made = [jax.ShapeDtypeStruct(s, F32) for s in (shapes if many else [shapes])]
+    made = [pltpu.VMEM(s, F32) for s in (shapes if many else [shapes])]
     return pl.pallas_call(
         kernel,
         out_shape=made if many else made[0],
         in_specs=in_specs,
         out_specs=[VMEM] * len(made) if many else VMEM,
         scratch_shapes=list(scratch),
-        compiler_params=pltpu.CompilerParams(vmem_limit_bytes=48 * 2**20),
+        compiler_params=pltpu.CompilerParams(vmem_limit_bytes=room * 2**20),
         cost_estimate=pl.CostEstimate(flops=flops, bytes_accessed=2**20, transcendentals=0),
         name=name,
     )
@@ -202,8 +236,6 @@
     fields = control_raw.shape[1]
     square = (states, states)
     product = 12 * states**3
-    block = states // pattern.shape[0]
-    mask = jnp.repeat(jnp.repeat(pattern, block, axis=0), block, axis=1).astype(F32)
     bits = segments.bit_length() - 1
     turn = bits // 2 if members == 2 else 0
 
@@ -215,10 +247,10 @@
         return place * members + member
 
     both = ("tm", "ens")
-    place = lax.axis_index("tm")
-    member = lax.axis_index("ens")
-    segment = jnp.where(member % 2 == 1, turned(place, 1), place)
-    digits = [((segment >> r) & 1).astype(jnp.int32).reshape(1) for r in range(bits)]
+
+    def digit(r):
+        shift = lax.rem(r + turn * lax.rem(lax.axis_index("ens"), 2), bits)
+        return lax.bitwise_and(lax.shift_right_logical(lax.axis_index("tm"), shift), 1)
 
     if turn:
         amplitude = lax.ppermute(
@@ -226,13 +258,30 @@
             both,
             [(flat(turned(p, e), e), flat(p, e)) for p in range(segments) for e in range(members)],
         )
-    control, step, pair, local, held = call(
+    base, control = call(
+        generator_kernel,
+        [square, (fields,) + square],
+        [SMEM] * 2 + [HBM] * 4,
+        "generators",
+        flops=2 * product,
+        scratch=[
+            pltpu.VMEM((1, states), F32),
+            pltpu.VMEM(square, F32),
+            pltpu.VMEM(square, F32),
+            pltpu.VMEM((fields,) + square, F32),
+            pltpu.VMEM(square, F32),
+            pltpu.SemaphoreType.DMA((3 + fields,)),
+        ],
+        room=60,
+    )(b1_scale, pattern, relax.reshape(1, states), drift_raw, member_drift[0], control_raw[0])
+    step, pair, local, held = call(
         step_kernel,
-        [(fields,) + square, (count,) + square, (halves,) + square, (max(halves - 1, 1),) + square, square],
-        [SMEM, SMEM] + [VMEM] * 5,
+        [(count,) + square, (halves,) + square, (max(halves - 1, 1),) + square, square],
+        [SMEM, VMEM, VMEM],
         "steps",
         flops=50 * product,
-    )(amplitude, b1_scale, mask, relax.reshape(1, states), drift_raw, member_drift[0], control_raw[0])
+        room=32,
+    )(amplitude, base, control)
 
     after = before = prefix = suffix = None
     for r in range(bits):
@@ -246,36 +295,53 @@
             prefix, suffix = call(
                 local_kernel, [(count,) + square] * 2, [VMEM] * 4, "local", flops=5 * product
             )(step, pair, local, held)
+            other, prefix, suffix = lax.optimization_barrier((other, prefix, suffix))
         if r < bits - 1:
-            held = call(join_kernel, square, [SMEM, VMEM, VMEM], "join", flops=product)(digits[r], held, other)
+            held = call(
+                functools.partial(join_kernel, functools.partial(digit, r)), square, [VMEM] * 2, "join", flops=product
+            )(held, other)
             if after is None:
                 after, before = call(
-                    first_reach_kernel, [square] * 2, [SMEM, VMEM], "reach_first", flops=product // 4
-                )(digits[r], other)
+                    functools.partial(first_reach_kernel, functools.partial(digit, r)),
+                    [square] * 2,
+                    [VMEM],
+                    "reach_first",
+                    flops=product // 4,
+                )(other)
             else:
                 after, before = call(
-                    reach_kernel, [square] * 2, [SMEM] + [VMEM] * 3, "reach", flops=product
-                )(digits[r], other, after, before)
+                    functools.partial(reach_kernel, functools.partial(digit, r)),
+                    [square] * 2,
+                    [VMEM] * 3,
+                    "reach",
+                    flops=product,
+                )(other, after, before)
     left, right = call(
-        sides_kernel,
+        functools.partial(sides_kernel, functools.partial(digit, bits - 1)),
         [(count,) + square] * 2,
-        [SMEM] + [VMEM] * 5,
+        [VMEM] * 5,
         "sides",
         flops=6 * product,
         scratch=[pltpu.VMEM(square, F32)] * 2,
-    )(digits[-1], target, after, before, suffix, prefix)
-    mine = call(gradient_kernel, (8, 128), [SMEM] + [VMEM] * 4, "gradient", flops=6 * product)(
-        b1_scale, other, left, right, control
+    )(target, after, before, suffix, prefix)
+    mine = call(gradient_kernel, (8, 128), [VMEM] * 4, "gradient", flops=6 * product)(
+        other, left, right, control
     )
     if turn:
         first = [(flat(p, 1), flat(turned(p, 1), 0)) for p in range(segments)]
         first += [(flat(p, 0), flat(p, 1)) for p in range(segments)]
         second = [(flat(p, 1), flat(turned(p, 1), 1)) for p in range(segments)]
         second += [(flat(p, 0), flat(p, 0)) for p in range(segments)]
-        total = lax.ppermute(mine, both, first) + lax.ppermute(mine, both, second)
+        both_terms = (lax.ppermute(mine, both, first), lax.ppermute(mine, both, second))
     else:
-        total = lax.psum(mine, "ens")
-    return (total[:fields, :count], total[0, count : count + 1])
+        both_terms = (lax.psum(mine, "ens"), jnp.zeros_like(mine))
+    gradient, fidelity = pl.pallas_call(
+        finish_kernel,
+        out_shape=[jax.ShapeDtypeStruct((fields, count), F32), jax.ShapeDtypeStruct((1, 1), F32)],
+        compiler_params=pltpu.CompilerParams(vmem_limit_bytes=2**20),
+        name="finish",
+    )(*both_terms)
+    return gradient, fidelity.reshape(1)
 
 
 def solution(mesh):

time: 67.6 us -> 57.7 us (0.85)
  local copies, waits for them, and re-layouts: 9.7 us -> 0.01 us
  other arithmetic: 0.69 us -> 0 us
    unnamed x18 -> x2, local copies, waits for them, and re-layouts: 8.13 us -> 0.01 us
    pallas_call x1, Pallas kernels: 3.16 us -> 1.84 us  [per_device(): call(local_kernel, [(count,) + square] * 2, [VMEM] * 4, 'local', flops=5...]
    pallas_call x9 -> x11, Pallas kernels: 18.4 us -> 19.7 us  [the longest x1 10.2 us: per_device(): call(step_kernel, [(count,) + square, (halves,) + square, (max(halves - 1...]
    ppermute x1, waiting for transfers between devices: 1.23 us -> 0.01 us  [per_device(): lax.ppermute(amplitude, both, [(flat(turned(p, e), e), flat(p, e)) for p...]
    slice x2 -> x0, local copies, waits for them, and re-layouts: 1.16 us -> none  [per_device(): return (total[:fields, :count], total[0, count:count + 1])]
    ppermute x4, starting transfers between devices: 0.22 us -> 0.93 us  [per_device(): other = lax.ppermute(held, both, pairs)]
    convert_element_type x1 -> x0, other arithmetic: 0.68 us -> none  [per_device(): jnp.repeat(jnp.repeat(pattern, block, axis=0), block, axis=1).astype(F32)]
  transfers between devices with their start and end apart: 7 -> 7, of which waited for: 5 -> 5; matrix products, arithmetic and copies ran while one was open for 2% -> 0% of each run, Pallas kernels for 11% -> 12%
where the time goes in v2:
time: 57.7 us; the launch traced here: 56.7 us
  waiting for transfers between devices  22.9 us (40%)
  Pallas kernels  21.5 us (37%)
  starting transfers between devices  10.9 us (19%)
  between operations  1.42 us (2%)
    ppermute x4, waiting for transfers between devices, per_device(): other = lax.ppermute(held, both, pairs)  19.7 us
    pallas_call x1, Pallas kernels, per_device(): call(step_kernel, [(count,) + square, (halves,) + square, (max(halves - 1...  10.2 us
    ppermute x1, starting transfers between devices, per_device(): lax.ppermute(amplitude, both, [(flat(turned(p, e), e), flat(p, e)) for p...  5.14 us
    ppermute x1, starting transfers between devices, per_device(): lax.ppermute(mine, both, second)  4.69 us
    ppermute x1, waiting for transfers between devices, per_device(): lax.ppermute(mine, both, second)  3.15 us
    pallas_call x1, Pallas kernels, per_device(): call(gradient_kernel, (8, 128), [VMEM] * 4, 'gradient', flops=6 * product)  2.51 us
    pallas_call x1, Pallas kernels, per_device(): call(generator_kernel, [square, (fields,) + square], [SMEM] * 2 + [HBM] *...  2.47 us
    pallas_call x1, Pallas kernels, per_device(): call(local_kernel, [(count,) + square] * 2, [VMEM] * 4, 'local', flops=5...  1.84 us
  transfers between devices with their start and end apart: 7, of which 5 were waited for; matrix products, arithmetic and copies ran while one was open for 0% of the time, Pallas kernels for 12%

profile of v2, /device:TPU:7, one launch (start us, length us, event | category | flops | bytes accessed | tf_op | source)
XLA Modules:
  0.0 56.7 jit_solution(3788824444306414653)
XLA Ops:
  0.6 5.1 %collective-permute-start = (f32[4,6]{1,0:T(4,128)}, f32[4,6]{1,0:T(4,128)S(1)}, u32[]{:S(2)}, u32[]{:S(2)}) collective-permute-start(f32[4,6]{1,0:T(4,128)} %param.13), channel_id=1, source_target_pairs={{0,0},{1,1},{2,2},{9,3},{4,4},{17,5},{6,6},{25,7},{8,8},{3,9},{10,... | collective-permute-start | bytes 296 | tf_op jit(solution)/shard_map/ppermute | solution.py:256
  6.4 2.5 %generators.1 = (f32[256,256]{1,0:T(8,128)S(1)}, f32[4,256,256]{2,1,0:T(8,128)S(1)}) custom-call(f32[1]{0:T(128)S(6)} %copy.10.strength, s32[4,4]{1,0:T(4,128)} %pattern.1, f32[1,256]{1,0:T(1,128)} %bitcast.6, f32[256,256]{1,0:T(8,128)} %drift_raw.1, f32[256,256]{1,0:T(8,128)} %bitcast.5, f32[4,256,256]{2,1,0:T(8,128)} %bitcast.4), custom_call_target="tpu_custom_call" | custom-call | flops 402653184 | bytes 1048576 | tf_op jit(solution)/shard_map/generators/pallas_call | solution.py:261
  8.9 0.0 collective-permute-done.amplitude
  8.9 10.2 %steps.1 = (f32[6,256,256]{2,1,0:T(8,128)S(1)}, f32[3,256,256]{2,1,0:T(8,128)S(1)}, f32[2,256,256]{2,1,0:T(8,128)S(1)}, f32[256,256]{1,0:T(8,128)S(1)}) custom-call(f32[4,6]{1,0:T(4,128)S(1)} %collective-permute-done.amplitude, f32[256,256]{1,0:T(8,128)S(1)} %get-tuple-element.23.base, f32[4,256,256]{2,1,0:T(8,128)S(1)} %get-tuple-element.24.control), custom_call_target="tpu_custom_call" | custom-call | flops 10066329600 | bytes 1048576 | tf_op jit(solution)/shard_map/steps/pallas_call | solution.py:277
  19.1 0.4 collective-permute-start.1
  19.5 1.8 %local.1 = (f32[6,256,256]{2,1,0:T(8,128)S(1)}, f32[6,256,256]{2,1,0:T(8,128)S(1)}) custom-call(f32[6,256,256]{2,1,0:T(8,128)S(1)} %get-tuple-element.26.step, f32[3,256,256]{2,1,0:T(8,128)S(1)} %get-tuple-element.27.pair, f32[2,256,256]{2,1,0:T(8,128)S(1)} %get-tuple-element.28.before, f32[256,256]{1,0:T(8,128)S(1)} %get-tuple-element.25.segment.held), custom_call_target="tpu_custom_call" | custom-call | flops 1006632960 | bytes 1048576 | tf_op jit(solution)/shard_map/local/pallas_call | solution.py:295
  21.4 3.1 %collective-permute-done.1.other = f32[256,256]{1,0:T(8,128)S(1)} collective-permute-done((f32[256,256]{1,0:T(8,128)S(1)}, f32[256,256]{1,0:T(8,128)S(1)}, u32[]{:S(2)}, u32[]{:S(2)}) %collective-permute-start.1) | collective-permute-done | bytes 262176 | tf_op jit(solution)/shard_map/ppermute | solution.py:293
  24.4 0.4 join.3.held
  24.8 0.0 copy-start
  24.9 0.4 collective-permute-start.2
  25.3 8.7 %collective-permute-done.2.other = f32[256,256]{1,0:T(8,128)S(1)} collective-permute-done((f32[256,256]{1,0:T(8,128)S(1)}, f32[256,256]{1,0:T(8,128)S(1)}, u32[]{:S(2)}, u32[]{:S(2)}) %collective-permute-start.2) | collective-permute-done | bytes 262176 | tf_op jit(solution)/shard_map/ppermute | solution.py:293
  34.0 0.4 join.4.held
  34.3 0.1 collective-permute-start.3
  34.4 5.2 %collective-permute-done.3.other = f32[256,256]{1,0:T(8,128)S(1)} collective-permute-done((f32[256,256]{1,0:T(8,128)S(1)}, f32[256,256]{1,0:T(8,128)S(1)}, u32[]{:S(2)}, u32[]{:S(2)}) %collective-permute-start.3) | collective-permute-done | bytes 262176 | tf_op jit(solution)/shard_map/ppermute | solution.py:293
  39.6 0.4 join.5
  40.0 0.1 collective-permute-start.4
  40.1 0.1 reach_first.1
  40.2 0.4 reach.2
  40.6 0.6 %reach.3 = (f32[256,256]{1,0:T(8,128)S(1)}, f32[256,256]{1,0:T(8,128)S(1)}) custom-call(f32[256,256]{1,0:T(8,128)S(1)} %collective-permute-done.3.other, f32[256,256]{1,0:T(8,128)S(1)} %get-tuple-element.34.after, f32[256,256]{1,0:T(8,128)S(1)} %get-tuple-element.35.before), custom_call_target="tpu_custom_call" | custom-call | flops 201326592 | bytes 1048576 | tf_op jit(solution)/shard_map/reach/pallas_call | solution.py:312
  41.2 0.0 copy-done
  41.2 1.7 %sides.1 = (f32[6,256,256]{2,1,0:T(8,128)S(1)}, f32[6,256,256]{2,1,0:T(8,128)S(1)}) custom-call(f32[256,256]{1,0:T(8,128)S(1)} %copy-done, f32[256,256]{1,0:T(8,128)S(1)} %get-tuple-element.36.after, f32[256,256]{1,0:T(8,128)S(1)} %get-tuple-element.37.before, f32[6,256,256]{2,1,0:T(8,128)S(1)} %get-tuple-element.38.suffix, ...), custom_call_target="tpu_custom_call" | custom-call | flops 1207959552 | bytes 1048576 | tf_op jit(solution)/shard_map/sides/pallas_call | solution.py:319
  42.8 2.8 %collective-permute-done.4.other = f32[256,256]{1,0:T(8,128)S(1)} collective-permute-done((f32[256,256]{1,0:T(8,128)S(1)}, f32[256,256]{1,0:T(8,128)S(1)}, u32[]{:S(2)}, u32[]{:S(2)}) %collective-permute-start.4) | collective-permute-done | bytes 262176 | tf_op jit(solution)/shard_map/ppermute | solution.py:293
  45.6 2.5 %gradient.1 = f32[8,128]{1,0:T(8,128)S(1)} custom-call(f32[256,256]{1,0:T(8,128)S(1)} %collective-permute-done.4.other, f32[6,256,256]{2,1,0:T(8,128)S(1)} %get-tuple-element.40.left, f32[6,256,256]{2,1,0:T(8,128)S(1)} %get-tuple-element.41.right, f32[4,256,256]{2,1,0:T(8,128)S(1)} %get-tuple-element.24.control), custom_call_target="tpu_custom_call" | custom-call | flops 1207959552 | bytes 1048576 | tf_op jit(solution)/shard_map/gradient/pallas_call | solution.py:327
  48.1 4.7 %collective-permute-start.6 = (f32[8,128]{1,0:T(8,128)S(1)}, f32[8,128]{1,0:T(8,128)S(1)}, u32[]{:S(2)}, u32[]{:S(2)}) collective-permute-start(f32[8,128]{1,0:T(8,128)S(1)} %gradient.1), channel_id=1, source_target_pairs={{1,1},{3,9},{5,17},{7,25},{9,3},{11,11},{13,19},{15,27},{17,5},{19... | collective-permute-start | bytes 12296 | tf_op jit(solution)/shard_map/ppermute | solution.py:335
  52.8 0.1 collective-permute-start.5
  52.9 3.1 %collective-permute-done.6.second = f32[8,128]{1,0:T(8,128)S(1)} collective-permute-done((f32[8,128]{1,0:T(8,128)S(1)}, f32[8,128]{1,0:T(8,128)S(1)}, u32[]{:S(2)}, u32[]{:S(2)}) %collective-permute-start.6) | collective-permute-done | bytes 4128 | tf_op jit(solution)/shard_map/ppermute | solution.py:335
  56.1 0.0 collective-permute-done.5.first
  56.1 0.6 %finish.1 = (f32[4,6]{1,0:T(4,128)}, f32[1,1]{1,0:T(1,128)}) custom-call(f32[8,128]{1,0:T(8,128)S(1)} %collective-permute-done.5.first, f32[8,128]{1,0:T(8,128)S(1)} %collective-permute-done.6.second), custom_call_target="tpu_custom_call" | custom-call | tf_op jit(solution)/shard_map/finish/pallas_call | solution.py:338
Async XLA Ops:
  0.6 8.3 %collective-permute-start = (f32[4,6]{1,0:T(4,128)}, f32[4,6]{1,0:T(4,128)S(1)}, u32[]{:S(2)}, u32[]{:S(2)}) collective-permute-start(f32[4,6]{1,0:T(4,128)} %param.13), channel_id=1, source_target_pairs={{0,0},{1,1},{2,2},{9,3},{4,4},{17,5},{6,6},{25,7},{8,8},{3,9},{10,... | collective-permute-start | bytes 296 | tf_op jit(solution)/shard_map/ppermute | solution.py:256
  19.1 5.3 %collective-permute-start.1 = (f32[256,256]{1,0:T(8,128)S(1)}, f32[256,256]{1,0:T(8,128)S(1)}, u32[]{:S(2)}, u32[]{:S(2)}) collective-permute-start(f32[256,256]{1,0:T(8,128)S(1)} %get-tuple-element.25.segment.held), channel_id=1, source_target_pairs={{0,2},{2,0},{4,6},{6,4},{8,10},{10,8},{12,14},{14,12},{16,18},{18,... | collective-permute-start | bytes 786440 | tf_op jit(solution)/shard_map/ppermute | solution.py:293
  24.8 16.3 %copy-start = (f32[256,256]{1,0:T(8,128)S(1)}, f32[256,256]{1,0:T(8,128)}, u32[]{:S(2)}) copy-start(f32[256,256]{1,0:T(8,128)} %target.1) | copy-start | bytes 786436
  24.9 9.1 %collective-permute-start.2 = (f32[256,256]{1,0:T(8,128)S(1)}, f32[256,256]{1,0:T(8,128)S(1)}, u32[]{:S(2)}, u32[]{:S(2)}) collective-permute-start(f32[256,256]{1,0:T(8,128)S(1)} %join.3.held), channel_id=1, source_target_pairs={{0,4},{2,6},{4,0},{6,2},{8,12},{10,14},{12,8},{14,10},{16,20},{18,... | collective-permute-start | bytes 786440 | tf_op jit(solution)/shard_map/ppermute | solution.py:293
  34.3 5.3 %collective-permute-start.3 = (f32[256,256]{1,0:T(8,128)S(1)}, f32[256,256]{1,0:T(8,128)S(1)}, u32[]{:S(2)}, u32[]{:S(2)}) collective-permute-start(f32[256,256]{1,0:T(8,128)S(1)} %join.4.held), channel_id=1, source_target_pairs={{0,8},{2,10},{4,12},{6,14},{8,0},{10,2},{12,4},{14,6},{16,24},{18,... | collective-permute-start | bytes 786440 | tf_op jit(solution)/shard_map/ppermute | solution.py:293
  40.0 5.6 %collective-permute-start.4 = (f32[256,256]{1,0:T(8,128)S(1)}, f32[256,256]{1,0:T(8,128)S(1)}, u32[]{:S(2)}, u32[]{:S(2)}) collective-permute-start(f32[256,256]{1,0:T(8,128)S(1)} %join.5), channel_id=1, source_target_pairs={{0,16},{2,18},{4,20},{6,22},{8,24},{10,26},{12,28},{14,30},{16,0},... | collective-permute-start | bytes 786440 | tf_op jit(solution)/shard_map/ppermute | solution.py:293
  48.1 7.9 %collective-permute-start.6 = (f32[8,128]{1,0:T(8,128)S(1)}, f32[8,128]{1,0:T(8,128)S(1)}, u32[]{:S(2)}, u32[]{:S(2)}) collective-permute-start(f32[8,128]{1,0:T(8,128)S(1)} %gradient.1), channel_id=1, source_target_pairs={{1,1},{3,9},{5,17},{7,25},{9,3},{11,11},{13,19},{15,27},{17,5},{19... | collective-permute-start | bytes 12296 | tf_op jit(solution)/shard_map/ppermute | solution.py:335
  52.8 3.3 %collective-permute-start.5 = (f32[8,128]{1,0:T(8,128)S(1)}, f32[8,128]{1,0:T(8,128)S(1)}, u32[]{:S(2)}, u32[]{:S(2)}) collective-permute-start(f32[8,128]{1,0:T(8,128)S(1)} %gradient.1), channel_id=1, source_target_pairs={{1,0},{3,8},{5,16},{7,24},{9,2},{11,10},{13,18},{15,26},{17,4},{19... | collective-permute-start | bytes 12296 | tf_op jit(solution)/shard_map/ppermute | solution.py:335

commit v3 on v2

--- a/solution.py
+++ b/solution.py
@@ -54,7 +54,7 @@
 
 def exponents(scaled):
     second = [six(x, x) for x in scaled]
-    third = [six(x, y) for x, y in zip(scaled, second)]
+    third = [three(x, y) for x, y in zip(scaled, second)]
     rest = [
         x + y * 0.5 + z * (1.0 / 6) + three(z, x * (1.0 / 24) + y * (1.0 / 120) + z * (1.0 / 720))
         for x, y, z in zip(scaled, second, third)
@@ -151,11 +151,14 @@
     joined[...] = six(jnp.where(upper, mine, theirs), jnp.where(upper, theirs, mine))
 
 
-def first_reach_kernel(place, other, after_out, before_out):
-    upper = place() == 1
+def first_reach_kernel(first_place, place, first, other, after_out, before_out):
+    first_upper, upper = first_place() == 1, place() == 1
     eye = unit(other.shape[0])
-    after_out[...] = jnp.where(upper, eye, other[...])
-    before_out[...] = jnp.where(upper, other[...], eye)
+    after = jnp.where(first_upper, eye, first[...])
+    before = jnp.where(first_upper, first[...], eye)
+    product = six(jnp.where(upper, before, other[...]), jnp.where(upper, other[...], after))
+    after_out[...] = jnp.where(upper, after, product)
+    before_out[...] = jnp.where(upper, product, before)
 
 
 def reach_kernel(place, other, after, before, after_out, before_out):
@@ -166,7 +169,7 @@
 
 
 def sides_kernel(place, target, after, before, suffix, prefix, left_out, right_out, left, right):
-    count = prefix.shape[0]
+    count, states = prefix.shape[0], prefix.shape[1]
     bit = place()
 
     @pl.when(bit == 1)
@@ -180,41 +183,64 @@
         right[...] = three(target[...], before[...], NT)
 
     for k in range(count):
-        left_out[k] = three(suffix[k], left[...], TN) if k < count - 1 else left[...]
-        right_out[k] = three(right[...], prefix[k], NT)
+        lead, rest = parts(three(suffix[k], left[...], TN) if k < count - 1 else left[...], 2)
+        rows = slice(k * states, (k + 1) * states)
+        for place_, part in enumerate((lead, rest, lead)):
+            left_out[rows, place_ * states : (place_ + 1) * states] = part
+        lead, rest = parts(three(right[...], prefix[k], NT), 2)
+        for place_, part in enumerate((lead, lead, rest)):
+            right_out[k, place_ * states : (place_ + 1) * states] = part
 
 
 def gradient_kernel(other, left, right, control, out):
-    count, states = left.shape[0], left.shape[1]
+    count, states = right.shape[0], right.shape[2]
     fields = control.shape[0]
-    middle = three(left[...].reshape(count * states, states), other[...], NT)
-    lane = lax.broadcasted_iota(jnp.int32, out.shape, 1)
-    line = lax.broadcasted_iota(jnp.int32, out.shape, 0)
+    lanes = out.shape[1]
+    lead, rest = parts(other[...], 2)
+    other_parts = jnp.concatenate([lead, lead, rest], axis=1)
     row = lax.broadcasted_iota(jnp.int32, (states, states), 0)
     column = lax.broadcasted_iota(jnp.int32, (states, states), 1)
-    total = jnp.zeros(out.shape, F32)
+    lane = lax.broadcasted_iota(jnp.int32, (8, lanes), 1)
+    line = lax.broadcasted_iota(jnp.int32, (8, lanes), 0)
+
+    def fold(value):
+        rows = jnp.sum(value.reshape(states // 8, 8, states), axis=0)
+        return sum(rows[:, start : start + lanes] for start in range(0, states, lanes))
+
     overlap = None
-    for k in range(count):
-        projected = three(middle[k * states : (k + 1) * states], right[k])
+    tiles = []
+    for k in reversed(range(count)):
+        middle = dot(left[k * states : (k + 1) * states], other_parts, NT)
+        lead, rest = parts(middle, 2)
+        projected = dot(jnp.concatenate([lead, rest, lead], axis=1), right[k])
         if k == count - 1:
-            overlap = jnp.sum(jnp.where(row == column, projected, 0.0))
+            overlap = jnp.sum(fold(jnp.where(row == column, projected, 0.0)))
+        tile = jnp.zeros((8, lanes), F32)
         for c in range(fields):
-            term = jnp.sum(control[c] * projected)
-            total = jnp.where((line == c) & (lane == k), term, total)
-    total = total * (2.0 * overlap)
-    out[...] = jnp.where((line == 0) & (lane == count), overlap * overlap, total)
+            term = jnp.sum(fold(control[c] * projected), axis=0, keepdims=True)
+            tile = jnp.where(line == c, term, tile)
+        tiles.append((k, tile))
+    for k, tile in tiles:
+        out[8 * k : 8 * k + 8] = tile * (2.0 * overlap)
+    out[8 * count : 8 * count + 8] = jnp.where((lane == 0) & (line == 0), overlap * overlap, 0.0)
 
 
 def finish_kernel(first, second, gradient_out, fidelity_out):
     fields, count = gradient_out.shape
-    total = first[...] + second[...]
-    gradient_out[...] = total[:fields, :count]
-    fidelity_out[...] = total[:1, count : count + 1]
-
-
-def call(kernel, shapes, in_specs, name, flops=0, scratch=(), room=12):
+    lane = lax.broadcasted_iota(jnp.int32, (8, count), 1)
+    total = jnp.zeros((8, count), F32)
+    for k in range(count):
+        rows = slice(8 * k, 8 * k + 8)
+        term = jnp.sum(first[rows] + second[rows], axis=1, keepdims=True)
+        total = jnp.where(lane == k, term, total)
+    gradient_out[...] = total[:fields]
+    last = slice(8 * count, 8 * count + 1)
+    fidelity_out[...] = (first[last] + second[last])[:, :1]
+
+
+def call(kernel, shapes, in_specs, name, flops=0, scratch=(), room=12, dtype=F32):
     many = isinstance(shapes, list)
-    made = [pltpu.VMEM(s, F32) for s in (shapes if many else [shapes])]
+    made = [pltpu.VMEM(s, dtype) for s in (shapes if many else [shapes])]
     return pl.pallas_call(
         kernel,
         out_shape=made if many else made[0],
@@ -283,12 +309,15 @@
         room=32,
     )(amplitude, base, control)
 
-    after = before = prefix = suffix = None
+    prefix = suffix = after = before = None
+    others = []
     for r in range(bits):
         pairs = []
         for e in range(members):
-            shift = turn if e % 2 else 0
-            flip = 1 << ((r + shift) % bits)
+            top = (r + (turn if e % 2 else 0)) % bits
+            flip = 1 << top
+            if top == bits - 1 and (r > 0):
+                flip |= flip >> 1
             pairs += [(flat(p, e), flat(p ^ flip, e)) for p in range(segments)]
         other = lax.ppermute(held, both, pairs)
         if r == 0:
@@ -296,35 +325,37 @@
                 local_kernel, [(count,) + square] * 2, [VMEM] * 4, "local", flops=5 * product
             )(step, pair, local, held)
             other, prefix, suffix = lax.optimization_barrier((other, prefix, suffix))
+        if r >= 2:
+            known = [functools.partial(digit, r - 1)]
+            if r == 2:
+                after, before = call(
+                    functools.partial(first_reach_kernel, functools.partial(digit, 0), *known),
+                    [square] * 2,
+                    [VMEM] * 2,
+                    "reach_first",
+                    flops=product,
+                )(*others)
+            else:
+                after, before = call(
+                    functools.partial(reach_kernel, *known), [square] * 2, [VMEM] * 3, "reach", flops=product
+                )(others[-1], after, before)
+            if r < bits - 1:
+                other, after, before = lax.optimization_barrier((other, after, before))
+        others.append(other)
         if r < bits - 1:
             held = call(
                 functools.partial(join_kernel, functools.partial(digit, r)), square, [VMEM] * 2, "join", flops=product
             )(held, other)
-            if after is None:
-                after, before = call(
-                    functools.partial(first_reach_kernel, functools.partial(digit, r)),
-                    [square] * 2,
-                    [VMEM],
-                    "reach_first",
-                    flops=product // 4,
-                )(other)
-            else:
-                after, before = call(
-                    functools.partial(reach_kernel, functools.partial(digit, r)),
-                    [square] * 2,
-                    [VMEM] * 3,
-                    "reach",
-                    flops=product,
-                )(other, after, before)
     left, right = call(
         functools.partial(sides_kernel, functools.partial(digit, bits - 1)),
-        [(count,) + square] * 2,
+        [(count * states, 3 * states), (count, 3 * states, states)],
         [VMEM] * 5,
         "sides",
         flops=6 * product,
+        dtype=BF16,
         scratch=[pltpu.VMEM(square, F32)] * 2,
     )(target, after, before, suffix, prefix)
-    mine = call(gradient_kernel, (8, 128), [VMEM] * 4, "gradient", flops=6 * product)(
+    mine = call(gradient_kernel, (8 * count + 8, 128), [VMEM] * 4, "gradient", flops=6 * product)(
         other, left, right, control
     )
     if turn:

time: 57.7 us -> 54.6 us (0.946)
  waiting for transfers between devices: 22.9 us -> 20.9 us
  Pallas kernels: 21.5 us -> 20.5 us
    ppermute x4, waiting for transfers between devices: 19.7 us -> 17.8 us  [per_device(): other = lax.ppermute(held, both, pairs)]
    pallas_call x4 -> x3, Pallas kernels: 3.54 us -> 2.84 us  [the longest x1 2.04 us: per_device(): call(gradient_kernel, (8 * count + 8, 128), [VMEM] * 4, 'gradient', flops...]
  transfers between devices with their start and end apart: 7 -> 7, of which waited for: 5 -> 5; matrix products, arithmetic and copies ran while one was open for 0% -> 0% of each run, Pallas kernels for 12% -> 13%
where the time goes in v3:
time: 54.6 us; the launch traced here: 54 us
  waiting for transfers between devices  20.9 us (38%)
  Pallas kernels  20.5 us (38%)
  starting transfers between devices  11.1 us (20%)
  between operations  1.42 us (3%)
    ppermute x4, waiting for transfers between devices, per_device(): other = lax.ppermute(held, both, pairs)  17.8 us
    pallas_call x1, Pallas kernels, per_device(): call(step_kernel, [(count,) + square, (halves,) + square, (max(halves - 1...  9.64 us
    ppermute x1, starting transfers between devices, per_device(): lax.ppermute(amplitude, both, [(flat(turned(p, e), e), flat(p, e)) for p...  5.14 us
    ppermute x1, starting transfers between devices, per_device(): lax.ppermute(mine, both, second)  4.99 us
    ppermute x1, waiting for transfers between devices, per_device(): lax.ppermute(mine, both, second)  3.15 us
    pallas_call x1, Pallas kernels, per_device(): call(generator_kernel, [square, (fields,) + square], [SMEM] * 2 + [HBM] *...  2.47 us
    pallas_call x1, Pallas kernels, per_device(): call(gradient_kernel, (8 * count + 8, 128), [VMEM] * 4, 'gradient', flops...  2.04 us
    pallas_call x1, Pallas kernels, per_device(): call(functools.partial(sides_kernel, functools.partial(digit, bits - 1)),...  1.92 us
  transfers between devices with their start and end apart: 7, of which 5 were waited for; matrix products, arithmetic and copies ran while one was open for 0% of the time, Pallas kernels for 13%

profile of v3, /device:TPU:7, one launch (start us, length us, event | category | flops | bytes accessed | tf_op | source)
XLA Modules:
  0.0 54.0 jit_solution(13688207525367273355)
XLA Ops:
  0.6 5.1 %collective-permute-start = (f32[4,6]{1,0:T(4,128)}, f32[4,6]{1,0:T(4,128)S(1)}, u32[]{:S(2)}, u32[]{:S(2)}) collective-permute-start(f32[4,6]{1,0:T(4,128)} %param.13), channel_id=1, source_target_pairs={{0,0},{1,1},{2,2},{9,3},{4,4},{17,5},{6,6},{25,7},{8,8},{3,9},{10,... | collective-permute-start | bytes 296 | tf_op jit(solution)/shard_map/ppermute | solution.py:282
  6.4 2.5 %generators.1 = (f32[256,256]{1,0:T(8,128)S(1)}, f32[4,256,256]{2,1,0:T(8,128)S(1)}) custom-call(f32[1]{0:T(128)S(6)} %copy.10.strength, s32[4,4]{1,0:T(4,128)} %pattern.1, f32[1,256]{1,0:T(1,128)} %bitcast.6, f32[256,256]{1,0:T(8,128)} %drift_raw.1, f32[256,256]{1,0:T(8,128)} %bitcast.5, f32[4,256,256]{2,1,0:T(8,128)} %bitcast.4), custom_call_target="tpu_custom_call" | custom-call | flops 402653184 | bytes 1048576 | tf_op jit(solution)/shard_map/generators/pallas_call | solution.py:287
  8.9 0.0 collective-permute-done.amplitude
  8.9 9.6 %steps.1 = (f32[6,256,256]{2,1,0:T(8,128)S(1)}, f32[3,256,256]{2,1,0:T(8,128)S(1)}, f32[2,256,256]{2,1,0:T(8,128)S(1)}, f32[256,256]{1,0:T(8,128)S(1)}) custom-call(f32[4,6]{1,0:T(4,128)S(1)} %collective-permute-done.amplitude, f32[256,256]{1,0:T(8,128)S(1)} %get-tuple-element.24.base, f32[4,256,256]{2,1,0:T(8,128)S(1)} %get-tuple-element.25.control), custom_call_target="tpu_custom_call" | custom-call | flops 10066329600 | bytes 1048576 | tf_op jit(solution)/shard_map/steps/pallas_call | solution.py:303
  18.6 0.4 collective-permute-start.1
  18.9 1.8 %local.1 = (f32[6,256,256]{2,1,0:T(8,128)S(1)}, f32[6,256,256]{2,1,0:T(8,128)S(1)}) custom-call(f32[6,256,256]{2,1,0:T(8,128)S(1)} %get-tuple-element.27.step, f32[3,256,256]{2,1,0:T(8,128)S(1)} %get-tuple-element.28.pair, f32[2,256,256]{2,1,0:T(8,128)S(1)} %get-tuple-element.29.before, f32[256,256]{1,0:T(8,128)S(1)} %get-tuple-element.26.segment.held), custom_call_target="tpu_custom_call" | custom-call | flops 1006632960 | bytes 1048576 | tf_op jit(solution)/shard_map/local/pallas_call | solution.py:324
  20.8 3.1 %collective-permute-done.1.other.first = f32[256,256]{1,0:T(8,128)S(1)} collective-permute-done((f32[256,256]{1,0:T(8,128)S(1)}, f32[256,256]{1,0:T(8,128)S(1)}, u32[]{:S(2)}, u32[]{:S(2)}) %collective-permute-start.1) | collective-permute-done | bytes 262176 | tf_op jit(solution)/shard_map/ppermute | solution.py:322
  23.9 0.4 join.3.held
  24.3 0.0 copy-start
  24.3 0.4 collective-permute-start.2
  24.7 6.8 %collective-permute-done.2.other = f32[256,256]{1,0:T(8,128)S(1)} collective-permute-done((f32[256,256]{1,0:T(8,128)S(1)}, f32[256,256]{1,0:T(8,128)S(1)}, u32[]{:S(2)}, u32[]{:S(2)}) %collective-permute-start.2) | collective-permute-done | bytes 262176 | tf_op jit(solution)/shard_map/ppermute | solution.py:322
  31.5 0.4 join.4.held
  31.9 0.1 collective-permute-start.3
  31.9 0.4 reach_first.1
  32.3 4.8 %collective-permute-done.3.other = f32[256,256]{1,0:T(8,128)S(1)} collective-permute-done((f32[256,256]{1,0:T(8,128)S(1)}, f32[256,256]{1,0:T(8,128)S(1)}, u32[]{:S(2)}, u32[]{:S(2)}) %collective-permute-start.3) | collective-permute-done | bytes 262176 | tf_op jit(solution)/shard_map/ppermute | solution.py:322
  37.1 0.4 join.5
  37.5 0.1 collective-permute-start.4
  37.6 0.4 reach.1
  38.0 0.0 copy-done
  38.0 1.9 %sides.1 = (bf16[1536,768]{1,0:T(8,128)(2,1)S(1)}, bf16[6,768,256]{2,1,0:T(8,128)(2,1)S(1)}) custom-call(f32[256,256]{1,0:T(8,128)S(1)} %copy-done, f32[256,256]{1,0:T(8,128)S(1)} %get-tuple-element.38.after, f32[256,256]{1,0:T(8,128)S(1)} %get-tuple-element.39.before, f32[6,256,256]{2,1,0:T(8,128)S(1)} %get-tuple-element.40.suffix, ...), custom_call_target="tpu_custom_call" | custom-call | flops 1207959552 | bytes 1048576 | tf_op jit(solution)/shard_map/sides/pallas_call | solution.py:349
  40.0 3.2 %collective-permute-done.4.other = f32[256,256]{1,0:T(8,128)S(1)} collective-permute-done((f32[256,256]{1,0:T(8,128)S(1)}, f32[256,256]{1,0:T(8,128)S(1)}, u32[]{:S(2)}, u32[]{:S(2)}) %collective-permute-start.4) | collective-permute-done | bytes 262176 | tf_op jit(solution)/shard_map/ppermute | solution.py:322
  43.1 2.0 %gradient.1 = f32[56,128]{1,0:T(8,128)S(1)} custom-call(f32[256,256]{1,0:T(8,128)S(1)} %collective-permute-done.4.other, bf16[1536,768]{1,0:T(8,128)(2,1)S(1)} %get-tuple-element.42.left, bf16[6,768,256]{2,1,0:T(8,128)(2,1)S(1)} %get-tuple-element.43.right, f32[4,256,256]{2,1,0:T(8,128)S(1)} %get-tuple-element.25.control), custom_call_target="tpu_custom_call" | custom-call | flops 1207959552 | bytes 1048576 | tf_op jit(solution)/shard_map/gradient/pallas_call | solution.py:358
  45.2 5.0 %collective-permute-start.6 = (f32[56,128]{1,0:T(8,128)S(1)}, f32[56,128]{1,0:T(8,128)S(1)}, u32[]{:S(2)}, u32[]{:S(2)}) collective-permute-start(f32[56,128]{1,0:T(8,128)S(1)} %gradient.1), channel_id=1, source_target_pairs={{1,1},{3,9},{5,17},{7,25},{9,3},{11,11},{13,19},{15,27},{17,5},{19... | collective-permute-start | bytes 86024 | tf_op jit(solution)/shard_map/ppermute | solution.py:366
  50.2 0.1 collective-permute-start.5
  50.2 3.1 %collective-permute-done.6.second = f32[56,128]{1,0:T(8,128)S(1)} collective-permute-done((f32[56,128]{1,0:T(8,128)S(1)}, f32[56,128]{1,0:T(8,128)S(1)}, u32[]{:S(2)}, u32[]{:S(2)}) %collective-permute-start.6) | collective-permute-done | bytes 28704 | tf_op jit(solution)/shard_map/ppermute | solution.py:366
  53.4 0.0 collective-permute-done.5.first
  53.4 0.7 %finish.1 = (f32[4,6]{1,0:T(4,128)}, f32[1,1]{1,0:T(1,128)}) custom-call(f32[56,128]{1,0:T(8,128)S(1)} %collective-permute-done.5.first, f32[56,128]{1,0:T(8,128)S(1)} %collective-permute-done.6.second), custom_call_target="tpu_custom_call" | custom-call | tf_op jit(solution)/shard_map/finish/pallas_call | solution.py:369
Async XLA Ops:
  0.6 8.3 %collective-permute-start = (f32[4,6]{1,0:T(4,128)}, f32[4,6]{1,0:T(4,128)S(1)}, u32[]{:S(2)}, u32[]{:S(2)}) collective-permute-start(f32[4,6]{1,0:T(4,128)} %param.13), channel_id=1, source_target_pairs={{0,0},{1,1},{2,2},{9,3},{4,4},{17,5},{6,6},{25,7},{8,8},{3,9},{10,... | collective-permute-start | bytes 296 | tf_op jit(solution)/shard_map/ppermute | solution.py:282
  18.6 5.3 %collective-permute-start.1 = (f32[256,256]{1,0:T(8,128)S(1)}, f32[256,256]{1,0:T(8,128)S(1)}, u32[]{:S(2)}, u32[]{:S(2)}) collective-permute-start(f32[256,256]{1,0:T(8,128)S(1)} %get-tuple-element.26.segment.held), channel_id=1, source_target_pairs={{0,2},{2,0},{4,6},{6,4},{8,10},{10,8},{12,14},{14,12},{16,18},{18,... | collective-permute-start | bytes 786440 | tf_op jit(solution)/shard_map/ppermute | solution.py:322
  24.3 13.8 %copy-start = (f32[256,256]{1,0:T(8,128)S(1)}, f32[256,256]{1,0:T(8,128)}, u32[]{:S(2)}) copy-start(f32[256,256]{1,0:T(8,128)} %target.1) | copy-start | bytes 786436
  24.3 7.2 %collective-permute-start.2 = (f32[256,256]{1,0:T(8,128)S(1)}, f32[256,256]{1,0:T(8,128)S(1)}, u32[]{:S(2)}, u32[]{:S(2)}) collective-permute-start(f32[256,256]{1,0:T(8,128)S(1)} %join.3.held), channel_id=1, source_target_pairs={{0,4},{2,6},{4,0},{6,2},{8,12},{10,14},{12,8},{14,10},{16,20},{18,... | collective-permute-start | bytes 786440 | tf_op jit(solution)/shard_map/ppermute | solution.py:322
  31.9 5.3 %collective-permute-start.3 = (f32[256,256]{1,0:T(8,128)S(1)}, f32[256,256]{1,0:T(8,128)S(1)}, u32[]{:S(2)}, u32[]{:S(2)}) collective-permute-start(f32[256,256]{1,0:T(8,128)S(1)} %join.4.held), channel_id=1, source_target_pairs={{0,8},{2,10},{4,12},{6,14},{8,0},{10,2},{12,4},{14,6},{16,24},{18,... | collective-permute-start | bytes 786440 | tf_op jit(solution)/shard_map/ppermute | solution.py:322
  37.5 5.6 %collective-permute-start.4 = (f32[256,256]{1,0:T(8,128)S(1)}, f32[256,256]{1,0:T(8,128)S(1)}, u32[]{:S(2)}, u32[]{:S(2)}) collective-permute-start(f32[256,256]{1,0:T(8,128)S(1)} %join.5), channel_id=1, source_target_pairs={{0,24},{2,26},{4,28},{6,30},{8,16},{10,18},{12,20},{14,22},{16,8},... | collective-permute-start | bytes 786440 | tf_op jit(solution)/shard_map/ppermute | solution.py:322
  45.2 8.2 %collective-permute-start.6 = (f32[56,128]{1,0:T(8,128)S(1)}, f32[56,128]{1,0:T(8,128)S(1)}, u32[]{:S(2)}, u32[]{:S(2)}) collective-permute-start(f32[56,128]{1,0:T(8,128)S(1)} %gradient.1), channel_id=1, source_target_pairs={{1,1},{3,9},{5,17},{7,25},{9,3},{11,11},{13,19},{15,27},{17,5},{19... | collective-permute-start | bytes 86024 | tf_op jit(solution)/shard_map/ppermute | solution.py:366
  50.2 3.2 %collective-permute-start.5 = (f32[56,128]{1,0:T(8,128)S(1)}, f32[56,128]{1,0:T(8,128)S(1)}, u32[]{:S(2)}, u32[]{:S(2)}) collective-permute-start(f32[56,128]{1,0:T(8,128)S(1)} %gradient.1), channel_id=1, source_target_pairs={{1,0},{3,8},{5,16},{7,24},{9,2},{11,10},{13,18},{15,26},{17,4},{19... | collective-permute-start | bytes 86024 | tf_op jit(solution)/shard_map/ppermute | solution.py:366

commit v4 on v3

--- a/solution.py
+++ b/solution.py
@@ -9,6 +9,7 @@
 
 ORDER = 6
 SQ = 3
+AHEAD = 2
 F32 = jnp.float32
 BF16 = jnp.bfloat16
 VMEM = pl.BlockSpec(memory_space=pltpu.VMEM)
@@ -33,11 +34,14 @@
     return lax.dot_general(first, second, dims, preferred_element_type=F32)
 
 
-def six(first, second, dims=NN):
+def six(first, second):
+    rows = first.shape[0]
     a1, a2, a3 = parts(first, 3)
     b1, b2, b3 = parts(second, 3)
-    small = dot(a1, b3, dims) + dot(a2, b2, dims) + dot(a3, b1, dims)
-    return dot(a1, b1, dims) + ((dot(a1, b2, dims) + dot(a2, b1, dims)) + small)
+    large = dot(jnp.concatenate([a1, a2, a3], axis=0), b1)
+    middle = dot(jnp.concatenate([a1, a2], axis=0), b2)
+    small = (large[2 * rows :] + middle[rows:]) + dot(a1, b3)
+    return large[:rows] + ((large[rows : 2 * rows] + middle[:rows]) + small)
 
 
 def three(first, second, dims=NN):
@@ -168,8 +172,21 @@
     before_out[...] = jnp.where(upper, product, before[...])
 
 
-def sides_kernel(place, target, after, before, suffix, prefix, left_out, right_out, left, right):
+def along(value, axis, order):
+    pair = parts(value, 2)
+    return jnp.concatenate([pair[i] for i in order], axis=axis)
+
+
+FIRST, SECOND = (0, 1, 0), (0, 0, 1)
+
+
+def sides_kernel(
+    place, target, after, before, suffix, prefix, control, weight_out, overlap_out, *rest
+):
+    *direct_out, left, right, fields_parts = rest
     count, states = prefix.shape[0], prefix.shape[1]
+    fields = control.shape[0]
+    ahead = weight_out.shape[0] // fields
     bit = place()
 
     @pl.when(bit == 1)
@@ -182,24 +199,32 @@
         left[...] = after[...].T
         right[...] = three(target[...], before[...], NT)
 
+    for c in range(fields):
+        fields_parts[c * states : (c + 1) * states] = along(control[c], 1, FIRST)
     for k in range(count):
-        lead, rest = parts(three(suffix[k], left[...], TN) if k < count - 1 else left[...], 2)
-        rows = slice(k * states, (k + 1) * states)
-        for place_, part in enumerate((lead, rest, lead)):
-            left_out[rows, place_ * states : (place_ + 1) * states] = part
-        lead, rest = parts(three(right[...], prefix[k], NT), 2)
-        for place_, part in enumerate((lead, lead, rest)):
-            right_out[k, place_ * states : (place_ + 1) * states] = part
-
-
-def gradient_kernel(other, left, right, control, out):
-    count, states = right.shape[0], right.shape[2]
-    fields = control.shape[0]
+        outer = three(suffix[k], left[...], TN) if k < count - 1 else left[...]
+        inner = three(right[...], prefix[k], NT)
+        if k == count - 1:
+            overlap_out[...] = three(inner, outer)
+        if k < ahead:
+            turned = dot(fields_parts[...], along(outer, 0, SECOND))
+            inner_parts = along(inner, 1, FIRST)
+            for c in range(fields):
+                weight_out[k * fields + c] = dot(
+                    inner_parts, along(turned[c * states : (c + 1) * states], 0, SECOND)
+                )
+        else:
+            left_out, right_out = direct_out
+            left_out[(k - ahead) * states : (k - ahead + 1) * states] = along(outer, 1, FIRST)
+            right_out[k - ahead] = along(inner, 0, SECOND)
+
+
+def gradient_kernel(other, control, weight, overlap_weight, *rest):
+    *direct, out = rest
+    states, fields = other.shape[0], control.shape[0]
+    ahead = weight.shape[0] // fields
+    count = out.shape[0] // 8 - 1
     lanes = out.shape[1]
-    lead, rest = parts(other[...], 2)
-    other_parts = jnp.concatenate([lead, lead, rest], axis=1)
-    row = lax.broadcasted_iota(jnp.int32, (states, states), 0)
-    column = lax.broadcasted_iota(jnp.int32, (states, states), 1)
     lane = lax.broadcasted_iota(jnp.int32, (8, lanes), 1)
     line = lax.broadcasted_iota(jnp.int32, (8, lanes), 0)
 
@@ -207,21 +232,19 @@
         rows = jnp.sum(value.reshape(states // 8, 8, states), axis=0)
         return sum(rows[:, start : start + lanes] for start in range(0, states, lanes))
 
-    overlap = None
-    tiles = []
-    for k in reversed(range(count)):
-        middle = dot(left[k * states : (k + 1) * states], other_parts, NT)
-        lead, rest = parts(middle, 2)
-        projected = dot(jnp.concatenate([lead, rest, lead], axis=1), right[k])
-        if k == count - 1:
-            overlap = jnp.sum(fold(jnp.where(row == column, projected, 0.0)))
+    received = other[...]
+    overlap = jnp.sum(fold(overlap_weight[...] * received))
+    received_parts = along(received, 1, SECOND) if direct else None
+    for k in range(count):
+        if k >= ahead:
+            left, right = direct
+            middle = dot(left[(k - ahead) * states : (k - ahead + 1) * states], received_parts, NT)
+            projected = dot(along(middle, 1, FIRST), right[k - ahead])
         tile = jnp.zeros((8, lanes), F32)
         for c in range(fields):
-            term = jnp.sum(fold(control[c] * projected), axis=0, keepdims=True)
-            tile = jnp.where(line == c, term, tile)
-        tiles.append((k, tile))
-    for k, tile in tiles:
-        out[8 * k : 8 * k + 8] = tile * (2.0 * overlap)
+            value = control[c] * projected if k >= ahead else weight[k * fields + c] * received
+            tile = jnp.where(line == c, jnp.sum(fold(value), axis=0, keepdims=True), tile)
+        out[8 * k : 8 * k + 8] = tile * ((2.0 if k >= ahead else -2.0) * overlap)
     out[8 * count : 8 * count + 8] = jnp.where((lane == 0) & (line == 0), overlap * overlap, 0.0)
 
 
@@ -238,9 +261,9 @@
     fidelity_out[...] = (first[last] + second[last])[:, :1]
 
 
-def call(kernel, shapes, in_specs, name, flops=0, scratch=(), room=12, dtype=F32):
+def call(kernel, shapes, in_specs, name, flops=0, scratch=(), room=12):
     many = isinstance(shapes, list)
-    made = [pltpu.VMEM(s, dtype) for s in (shapes if many else [shapes])]
+    made = [s if isinstance(s, pl.MemoryRef) else pltpu.VMEM(s, F32) for s in (shapes if many else [shapes])]
     return pl.pallas_call(
         kernel,
         out_shape=made if many else made[0],
@@ -265,9 +288,12 @@
     bits = segments.bit_length() - 1
     turn = bits // 2 if members == 2 else 0
 
+    low = (1 << turn) - 1
+
     def turned(place, member):
-        shift = turn if member % 2 else 0
-        return ((place >> shift) | (place << (bits - shift))) & (segments - 1)
+        if not turn or member % 2 == 0:
+            return place
+        return ((~place & low) << (bits - turn)) | (place >> turn)
 
     def flat(place, member):
         return place * members + member
@@ -275,8 +301,10 @@
     both = ("tm", "ens")
 
     def digit(r):
-        shift = lax.rem(r + turn * lax.rem(lax.axis_index("ens"), 2), bits)
-        return lax.bitwise_and(lax.shift_right_logical(lax.axis_index("tm"), shift), 1)
+        odd = lax.rem(lax.axis_index("ens"), 2) if turn else 0
+        shift = lax.rem(r + turn * odd, bits)
+        bit = lax.bitwise_and(lax.shift_right_logical(lax.axis_index("tm"), shift), 1)
+        return lax.bitwise_xor(bit, odd) if turn and r >= bits - turn else bit
 
     if turn:
         amplitude = lax.ppermute(
@@ -346,24 +374,30 @@
             held = call(
                 functools.partial(join_kernel, functools.partial(digit, r)), square, [VMEM] * 2, "join", flops=product
             )(held, other)
-    left, right = call(
+    ahead = min(AHEAD, count)
+    direct = count - ahead
+    shapes = [(fields * ahead,) + square, square]
+    if direct:
+        shapes += [
+            pltpu.VMEM((direct * states, 3 * states), BF16),
+            pltpu.VMEM((direct, 3 * states, states), BF16),
+        ]
+    weights = call(
         functools.partial(sides_kernel, functools.partial(digit, bits - 1)),
-        [(count * states, 3 * states), (count, 3 * states, states)],
-        [VMEM] * 5,
+        shapes,
+        [VMEM] * 6,
         "sides",
-        flops=6 * product,
-        dtype=BF16,
-        scratch=[pltpu.VMEM(square, F32)] * 2,
-    )(target, after, before, suffix, prefix)
-    mine = call(gradient_kernel, (8 * count + 8, 128), [VMEM] * 4, "gradient", flops=6 * product)(
-        other, left, right, control
-    )
+        flops=20 * product,
+        scratch=[pltpu.VMEM(square, F32)] * 2 + [pltpu.VMEM((fields * states, 3 * states), BF16)],
+        room=20,
+    )(target, after, before, suffix, prefix, control)
+    mine = call(
+        gradient_kernel, (8 * count + 8, 128), [VMEM] * (2 + len(weights)), "gradient", flops=3 * product
+    )(other, control, *weights)
     if turn:
-        first = [(flat(p, 1), flat(turned(p, 1), 0)) for p in range(segments)]
-        first += [(flat(p, 0), flat(p, 1)) for p in range(segments)]
-        second = [(flat(p, 1), flat(turned(p, 1), 1)) for p in range(segments)]
-        second += [(flat(p, 0), flat(p, 0)) for p in range(segments)]
-        both_terms = (lax.ppermute(mine, both, first), lax.ppermute(mine, both, second))
+        home = [(flat(p, e), flat(turned(p, e), e)) for p in range(segments) for e in range(members)]
+        mine = lax.ppermute(mine, both, home)
+        both_terms = (mine, lax.ppermute(mine, "ens", [(0, 1), (1, 0)]))
     else:
         both_terms = (lax.psum(mine, "ens"), jnp.zeros_like(mine))
     gradient, fidelity = pl.pallas_call(

time: 54.6 us -> 53.5 us (0.980)
  Pallas kernels: 20.5 us -> 22.3 us
  waiting for transfers between devices: 20.9 us -> 19.2 us
  starting transfers between devices: 11.1 us -> 9.88 us
    ppermute x4, waiting for transfers between devices: 17.8 us -> 14.2 us  [per_device(): other = lax.ppermute(held, both, pairs)]
    pallas_call x1, Pallas kernels: 1.92 us -> 4.5 us  [per_device(): call(functools.partial(sides_kernel, functools.partial(digit, bits - 1)),...]
    ppermute x2, starting transfers between devices: 5.05 us -> 2.68 us  [the longest x1 2.68 us: per_device(): mine = lax.ppermute(mine, both, home)]
    ppermute x2, waiting for transfers between devices: 3.15 us -> 4.93 us  [the longest x1 3.73 us: per_device(): mine = lax.ppermute(mine, both, home)]
    ppermute x4, starting transfers between devices: 0.94 us -> 1.97 us  [per_device(): other = lax.ppermute(held, both, pairs)]
  transfers between devices with their start and end apart: 7 -> 7, of which waited for: 5 -> 6; matrix products, arithmetic and copies ran while one was open for 0% -> 0% of each run, Pallas kernels for 13% -> 18%
where the time goes in v4:
time: 53.5 us; the launch traced here: 52.7 us
  Pallas kernels  22.3 us (42%)
  waiting for transfers between devices  19.2 us (36%)
  starting transfers between devices  9.88 us (18%)
  between operations  1.4 us (3%)
    ppermute x4, waiting for transfers between devices, per_device(): other = lax.ppermute(held, both, pairs)  14.2 us
    pallas_call x1, Pallas kernels, per_device(): call(step_kernel, [(count,) + square, (halves,) + square, (max(halves - 1...  9.21 us
    ppermute x1, starting transfers between devices, per_device(): lax.ppermute(amplitude, both, [(flat(turned(p, e), e), flat(p, e)) for p...  5.23 us
    pallas_call x1, Pallas kernels, per_device(): call(functools.partial(sides_kernel, functools.partial(digit, bits - 1)),...  4.5 us
    ppermute x1, waiting for transfers between devices, per_device(): mine = lax.ppermute(mine, both, home)  3.73 us
    ppermute x1, starting transfers between devices, per_device(): mine = lax.ppermute(mine, both, home)  2.68 us
    pallas_call x1, Pallas kernels, per_device(): call(generator_kernel, [square, (fields,) + square], [SMEM] * 2 + [HBM] *...  2.47 us
    ppermute x4, starting transfers between devices, per_device(): other = lax.ppermute(held, both, pairs)  1.97 us
  transfers between devices with their start and end apart: 7, of which 6 were waited for; matrix products, arithmetic and copies ran while one was open for 0% of the time, Pallas kernels for 18%

profile of v4, /device:TPU:7, one launch (start us, length us, event | category | flops | bytes accessed | tf_op | source)
XLA Modules:
  0.0 52.7 jit_solution(8814429295119845216)
XLA Ops:
  0.6 5.2 %collective-permute-start = (f32[4,6]{1,0:T(4,128)}, f32[4,6]{1,0:T(4,128)S(1)}, u32[]{:S(2)}, u32[]{:S(2)}) collective-permute-start(f32[4,6]{1,0:T(4,128)} %param.13), channel_id=1, source_target_pairs={{0,0},{25,1},{2,2},{17,3},{4,4},{9,5},{6,6},{1,7},{8,8},{27,9},{10... | collective-permute-start | bytes 296 | tf_op jit(solution)/shard_map/ppermute | solution.py:310
  6.5 2.5 %generators.1 = (f32[256,256]{1,0:T(8,128)S(1)}, f32[4,256,256]{2,1,0:T(8,128)S(1)}) custom-call(f32[1]{0:T(128)S(6)} %copy.10.strength, s32[4,4]{1,0:T(4,128)} %pattern.1, f32[1,256]{1,0:T(1,128)} %bitcast.6, f32[256,256]{1,0:T(8,128)} %drift_raw.1, f32[256,256]{1,0:T(8,128)} %bitcast.5, f32[4,256,256]{2,1,0:T(8,128)} %bitcast.4), custom_call_target="tpu_custom_call" | custom-call | flops 402653184 | bytes 1048576 | tf_op jit(solution)/shard_map/generators/pallas_call | solution.py:315
  9.0 0.0 collective-permute-done.amplitude
  9.0 9.2 %steps.1 = (f32[6,256,256]{2,1,0:T(8,128)S(1)}, f32[3,256,256]{2,1,0:T(8,128)S(1)}, f32[2,256,256]{2,1,0:T(8,128)S(1)}, f32[256,256]{1,0:T(8,128)S(1)}) custom-call(f32[4,6]{1,0:T(4,128)S(1)} %collective-permute-done.amplitude, f32[256,256]{1,0:T(8,128)S(1)} %get-tuple-element.26.base, f32[4,256,256]{2,1,0:T(8,128)S(1)} %get-tuple-element.27.control), custom_call_target="tpu_custom_call" | custom-call | flops 10066329600 | bytes 1048576 | tf_op jit(solution)/shard_map/steps/pallas_call | solution.py:331
  18.2 0.3 collective-permute-start.1
  18.5 1.8 %local.1 = (f32[6,256,256]{2,1,0:T(8,128)S(1)}, f32[6,256,256]{2,1,0:T(8,128)S(1)}) custom-call(f32[6,256,256]{2,1,0:T(8,128)S(1)} %get-tuple-element.29.step, f32[3,256,256]{2,1,0:T(8,128)S(1)} %get-tuple-element.30.pair, f32[2,256,256]{2,1,0:T(8,128)S(1)} %get-tuple-element.31.before, f32[256,256]{1,0:T(8,128)S(1)} %get-tuple-element.28.segment.held), custom_call_target="tpu_custom_call" | custom-call | flops 1006632960 | bytes 1048576 | tf_op jit(solution)/shard_map/local/pallas_call | solution.py:352
  20.3 3.2 %collective-permute-done.1.other.first = f32[256,256]{1,0:T(8,128)S(1)} collective-permute-done((f32[256,256]{1,0:T(8,128)S(1)}, f32[256,256]{1,0:T(8,128)S(1)}, u32[]{:S(2)}, u32[]{:S(2)}) %collective-permute-start.1) | collective-permute-done | bytes 262176 | tf_op jit(solution)/shard_map/ppermute | solution.py:350
  23.5 0.4 join.3.held
  23.9 0.0 copy-start
  23.9 1.3 %collective-permute-start.2 = (f32[256,256]{1,0:T(8,128)S(1)}, f32[256,256]{1,0:T(8,128)S(1)}, u32[]{:S(2)}, u32[]{:S(2)}) collective-permute-start(f32[256,256]{1,0:T(8,128)S(1)} %join.3.held), channel_id=1, source_target_pairs={{0,4},{2,6},{4,0},{6,2},{8,12},{10,14},{12,8},{14,10},{16,20},{18,... | collective-permute-start | bytes 786440 | tf_op jit(solution)/shard_map/ppermute | solution.py:350
  25.3 5.8 %collective-permute-done.2.other = f32[256,256]{1,0:T(8,128)S(1)} collective-permute-done((f32[256,256]{1,0:T(8,128)S(1)}, f32[256,256]{1,0:T(8,128)S(1)}, u32[]{:S(2)}, u32[]{:S(2)}) %collective-permute-start.2) | collective-permute-done | bytes 262176 | tf_op jit(solution)/shard_map/ppermute | solution.py:350
  31.1 0.4 join.4.held
  31.5 0.2 collective-permute-start.3
  31.8 0.4 reach_first.1
  32.2 4.6 %collective-permute-done.3.other = f32[256,256]{1,0:T(8,128)S(1)} collective-permute-done((f32[256,256]{1,0:T(8,128)S(1)}, f32[256,256]{1,0:T(8,128)S(1)}, u32[]{:S(2)}, u32[]{:S(2)}) %collective-permute-start.3) | collective-permute-done | bytes 262176 | tf_op jit(solution)/shard_map/ppermute | solution.py:350
  36.8 0.4 join.5
  37.2 0.1 collective-permute-start.4
  37.3 0.4 reach.1
  37.7 0.0 copy-done
  37.7 4.5 %sides.1 = (f32[8,256,256]{2,1,0:T(8,128)S(1)}, f32[256,256]{1,0:T(8,128)S(1)}, bf16[1024,768]{1,0:T(8,128)(2,1)S(1)}, bf16[4,768,256]{2,1,0:T(8,128)(2,1)S(1)}) custom-call(f32[256,256]{1,0:T(8,128)S(1)} %copy-done, f32[256,256]{1,0:T(8,128)S(1)} %get-tuple-element.40.after, f32[256,256]{1,0:T(8,128)S(1)} %get-tuple-element.41.before, ...), custom_call_target="tpu_custom_call" | custom-call | flops 4026531840 | bytes 1048576 | tf_op jit(solution)/shard_map/sides/pallas_call | solution.py:385
  42.2 0.6 %collective-permute-done.4.other = f32[256,256]{1,0:T(8,128)S(1)} collective-permute-done((f32[256,256]{1,0:T(8,128)S(1)}, f32[256,256]{1,0:T(8,128)S(1)}, u32[]{:S(2)}, u32[]{:S(2)}) %collective-permute-start.4) | collective-permute-done | bytes 262176 | tf_op jit(solution)/shard_map/ppermute | solution.py:350
  42.8 1.6 %gradient.1 = f32[56,128]{1,0:T(8,128)S(1)} custom-call(f32[256,256]{1,0:T(8,128)S(1)} %collective-permute-done.4.other, f32[4,256,256]{2,1,0:T(8,128)S(1)} %get-tuple-element.27.control, f32[8,256,256]{2,1,0:T(8,128)S(1)} %get-tuple-element.44.weight, f32[256,256]{1,0:T(8,128)S(1)} %get-tuple-element.45.overlap_weight, ...), custom_call_target="tpu_custom_call" | custom-call | flops 603979776 | bytes 1048576 | tf_op jit(solution)/shard_map/gradient/pallas_call | solution.py:394
  44.4 2.7 %collective-permute-start.5 = (f32[56,128]{1,0:T(8,128)S(1)}, f32[56,128]{1,0:T(8,128)S(1)}, u32[]{:S(2)}, u32[]{:S(2)}) collective-permute-start(f32[56,128]{1,0:T(8,128)S(1)} %gradient.1), channel_id=1, source_target_pairs={{0,0},{1,25},{2,2},{3,17},{4,4},{5,9},{6,6},{7,1},{8,8},{9,27},{10... | collective-permute-start | bytes 86024 | tf_op jit(solution)/shard_map/ppermute | solution.py:399
  47.1 3.7 %collective-permute-done.5.first = f32[56,128]{1,0:T(8,128)S(1)} collective-permute-done((f32[56,128]{1,0:T(8,128)S(1)}, f32[56,128]{1,0:T(8,128)S(1)}, u32[]{:S(2)}, u32[]{:S(2)}) %collective-permute-start.5) | collective-permute-done | bytes 28704 | tf_op jit(solution)/shard_map/ppermute | solution.py:399
  50.9 0.0 collective-permute-start.6
  50.9 1.2 %collective-permute-done.6.second = f32[56,128]{1,0:T(8,128)S(1)} collective-permute-done((f32[56,128]{1,0:T(8,128)S(1)}, f32[56,128]{1,0:T(8,128)S(1)}, u32[]{:S(2)}, u32[]{:S(2)}) %collective-permute-start.6) | collective-permute-done | bytes 28704 | tf_op jit(solution)/shard_map/ppermute | solution.py:400
  52.1 0.7 %finish.1 = (f32[4,6]{1,0:T(4,128)}, f32[1,1]{1,0:T(1,128)}) custom-call(f32[56,128]{1,0:T(8,128)S(1)} %collective-permute-done.5.first, f32[56,128]{1,0:T(8,128)S(1)} %collective-permute-done.6.second), custom_call_target="tpu_custom_call" | custom-call | tf_op jit(solution)/shard_map/finish/pallas_call | solution.py:403
Async XLA Ops:
  0.6 8.4 %collective-permute-start = (f32[4,6]{1,0:T(4,128)}, f32[4,6]{1,0:T(4,128)S(1)}, u32[]{:S(2)}, u32[]{:S(2)}) collective-permute-start(f32[4,6]{1,0:T(4,128)} %param.13), channel_id=1, source_target_pairs={{0,0},{25,1},{2,2},{17,3},{4,4},{9,5},{6,6},{1,7},{8,8},{27,9},{10... | collective-permute-start | bytes 296 | tf_op jit(solution)/shard_map/ppermute | solution.py:310
  18.2 5.3 %collective-permute-start.1 = (f32[256,256]{1,0:T(8,128)S(1)}, f32[256,256]{1,0:T(8,128)S(1)}, u32[]{:S(2)}, u32[]{:S(2)}) collective-permute-start(f32[256,256]{1,0:T(8,128)S(1)} %get-tuple-element.28.segment.held), channel_id=1, source_target_pairs={{0,2},{2,0},{4,6},{6,4},{8,10},{10,8},{12,14},{14,12},{16,18},{18,... | collective-permute-start | bytes 786440 | tf_op jit(solution)/shard_map/ppermute | solution.py:350
  23.9 13.8 %copy-start = (f32[256,256]{1,0:T(8,128)S(1)}, f32[256,256]{1,0:T(8,128)}, u32[]{:S(2)}) copy-start(f32[256,256]{1,0:T(8,128)} %target.1) | copy-start | bytes 786436
  23.9 7.2 %collective-permute-start.2 = (f32[256,256]{1,0:T(8,128)S(1)}, f32[256,256]{1,0:T(8,128)S(1)}, u32[]{:S(2)}, u32[]{:S(2)}) collective-permute-start(f32[256,256]{1,0:T(8,128)S(1)} %join.3.held), channel_id=1, source_target_pairs={{0,4},{2,6},{4,0},{6,2},{8,12},{10,14},{12,8},{14,10},{16,20},{18,... | collective-permute-start | bytes 786440 | tf_op jit(solution)/shard_map/ppermute | solution.py:350
  31.5 5.3 %collective-permute-start.3 = (f32[256,256]{1,0:T(8,128)S(1)}, f32[256,256]{1,0:T(8,128)S(1)}, u32[]{:S(2)}, u32[]{:S(2)}) collective-permute-start(f32[256,256]{1,0:T(8,128)S(1)} %join.4.held), channel_id=1, source_target_pairs={{0,8},{2,10},{4,12},{6,14},{8,0},{10,2},{12,4},{14,6},{16,24},{18,... | collective-permute-start | bytes 786440 | tf_op jit(solution)/shard_map/ppermute | solution.py:350
  37.2 5.6 %collective-permute-start.4 = (f32[256,256]{1,0:T(8,128)S(1)}, f32[256,256]{1,0:T(8,128)S(1)}, u32[]{:S(2)}, u32[]{:S(2)}) collective-permute-start(f32[256,256]{1,0:T(8,128)S(1)} %join.5), channel_id=1, source_target_pairs={{0,24},{2,26},{4,28},{6,30},{8,16},{10,18},{12,20},{14,22},{16,8},... | collective-permute-start | bytes 786440 | tf_op jit(solution)/shard_map/ppermute | solution.py:350
  44.4 6.4 %collective-permute-start.5 = (f32[56,128]{1,0:T(8,128)S(1)}, f32[56,128]{1,0:T(8,128)S(1)}, u32[]{:S(2)}, u32[]{:S(2)}) collective-permute-start(f32[56,128]{1,0:T(8,128)S(1)} %gradient.1), channel_id=1, source_target_pairs={{0,0},{1,25},{2,2},{3,17},{4,4},{5,9},{6,6},{7,1},{8,8},{9,27},{10... | collective-permute-start | bytes 86024 | tf_op jit(solution)/shard_map/ppermute | solution.py:399
  50.9 1.2 %collective-permute-start.6 = (f32[56,128]{1,0:T(8,128)S(1)}, f32[56,128]{1,0:T(8,128)S(1)}, u32[]{:S(2)}, u32[]{:S(2)}) collective-permute-start(f32[56,128]{1,0:T(8,128)S(1)} %collective-permute-done.5.first), channel_id=1, source_target_pairs={{0,1},{1,0},{2,3},{3,2},{4,5},{5,4},{6,7},{7,6},{8,9},{9,8},{10,11... | collective-permute-start | bytes 86024 | tf_op jit(solution)/shard_map/ppermute | solution.py:400

commit v5 on v4

--- a/solution.py
+++ b/solution.py
@@ -9,11 +9,9 @@
 
 ORDER = 6
 SQ = 3
-AHEAD = 2
 F32 = jnp.float32
 BF16 = jnp.bfloat16
 VMEM = pl.BlockSpec(memory_space=pltpu.VMEM)
-SMEM = pl.BlockSpec(memory_space=pltpu.SMEM)
 HBM = pl.BlockSpec(memory_space=pltpu.HBM)
 
 NN = (((1,), (0,)), ((), ()))
@@ -69,24 +67,26 @@
 
 
 def generator_kernel(
-    strength, pattern, relax, drift_raw, member_drift, control_raw, base_out, control_out,
-    relax_in, drift_in, member_in, control_in, coupled, arrived,
+    strength_raw, pattern_raw, relax, drift_raw, member_drift, control_raw, base_out, control_out,
+    strength, pattern, relax_in, drift_in, member_in, control_in, coupled, arrived,
 ):
     fields, states = control_raw.shape[0], control_raw.shape[1]
     moves = [
         pltpu.make_async_copy(drift_raw, drift_in, arrived.at[0]),
         pltpu.make_async_copy(member_drift, member_in, arrived.at[1]),
         pltpu.make_async_copy(relax, relax_in, arrived.at[2]),
+        pltpu.make_async_copy(pattern_raw, pattern, arrived.at[3]),
+        pltpu.make_async_copy(strength_raw, strength, arrived.at[4]),
     ]
     moves += [
-        pltpu.make_async_copy(control_raw.at[c], control_in.at[c], arrived.at[3 + c]) for c in range(fields)
+        pltpu.make_async_copy(control_raw.at[c], control_in.at[c], arrived.at[5 + c]) for c in range(fields)
     ]
     for move in moves:
         move.start()
     blocks = pattern.shape[0]
     size = states // blocks
     part = lax.broadcasted_iota(jnp.int32, (1, states), 1) // size
-    for move in moves[:3]:
+    for move in moves[:5]:
         move.wait()
     for i in range(blocks):
         line = jnp.zeros((1, states), F32)
@@ -98,8 +98,8 @@
     column = lax.broadcasted_iota(jnp.int32, (states, states), 1)
     base_out[...] = coupled[...] - coupled[...].T - jnp.where(row == column, relax_in[...], 0.0)
     for c in range(fields):
-        moves[3 + c].wait()
-        control_out[c] = strength[0] * (control_in[c] - control_in[c].T)
+        moves[5 + c].wait()
+        control_out[c] = strength[0, 0] * (control_in[c] - control_in[c].T)
 
 
 def step_kernel(amplitude, base, control, step_out, pair_out, before_out, segment_out):
@@ -108,9 +108,9 @@
     fields = control.shape[0]
     scaled = []
     for k in range(count):
-        field = amplitude[0, k] * control[0]
+        field = amplitude[:1, k : k + 1] * control[0]
         for c in range(1, fields):
-            field = field + amplitude[c, k] * control[c]
+            field = field + amplitude[c : c + 1, k : k + 1] * control[c]
         scaled.append((base[...] + field) * (1.0 / 2.0**SQ))
     eye = unit(states)
     steps = [eye + q for q in exponents(scaled)]
@@ -180,13 +180,8 @@
 FIRST, SECOND = (0, 1, 0), (0, 0, 1)
 
 
-def sides_kernel(
-    place, target, after, before, suffix, prefix, control, weight_out, overlap_out, *rest
-):
-    *direct_out, left, right, fields_parts = rest
+def sides_kernel(place, target, after, before, suffix, prefix, overlap_out, left_out, right_out, left, right):
     count, states = prefix.shape[0], prefix.shape[1]
-    fields = control.shape[0]
-    ahead = weight_out.shape[0] // fields
     bit = place()
 
     @pl.when(bit == 1)
@@ -199,31 +194,17 @@
         left[...] = after[...].T
         right[...] = three(target[...], before[...], NT)
 
-    for c in range(fields):
-        fields_parts[c * states : (c + 1) * states] = along(control[c], 1, FIRST)
     for k in range(count):
         outer = three(suffix[k], left[...], TN) if k < count - 1 else left[...]
         inner = three(right[...], prefix[k], NT)
         if k == count - 1:
             overlap_out[...] = three(inner, outer)
-        if k < ahead:
-            turned = dot(fields_parts[...], along(outer, 0, SECOND))
-            inner_parts = along(inner, 1, FIRST)
-            for c in range(fields):
-                weight_out[k * fields + c] = dot(
-                    inner_parts, along(turned[c * states : (c + 1) * states], 0, SECOND)
-                )
-        else:
-            left_out, right_out = direct_out
-            left_out[(k - ahead) * states : (k - ahead + 1) * states] = along(outer, 1, FIRST)
-            right_out[k - ahead] = along(inner, 0, SECOND)
-
-
-def gradient_kernel(other, control, weight, overlap_weight, *rest):
-    *direct, out = rest
-    states, fields = other.shape[0], control.shape[0]
-    ahead = weight.shape[0] // fields
-    count = out.shape[0] // 8 - 1
+        left_out[k * states : (k + 1) * states] = along(outer, 1, FIRST)
+        right_out[k] = along(inner, 0, SECOND)
+
+
+def gradient_kernel(other, control, overlap_weight, left, right, out):
+    states, fields, count = other.shape[0], control.shape[0], right.shape[0]
     lanes = out.shape[1]
     lane = lax.broadcasted_iota(jnp.int32, (8, lanes), 1)
     line = lax.broadcasted_iota(jnp.int32, (8, lanes), 0)
@@ -234,17 +215,14 @@
 
     received = other[...]
     overlap = jnp.sum(fold(overlap_weight[...] * received))
-    received_parts = along(received, 1, SECOND) if direct else None
-    for k in range(count):
-        if k >= ahead:
-            left, right = direct
-            middle = dot(left[(k - ahead) * states : (k - ahead + 1) * states], received_parts, NT)
-            projected = dot(along(middle, 1, FIRST), right[k - ahead])
+    received_parts = along(received, 1, SECOND)
+    for k in range(count):
+        middle = dot(left[k * states : (k + 1) * states], received_parts, NT)
+        projected = dot(along(middle, 1, FIRST), right[k])
         tile = jnp.zeros((8, lanes), F32)
         for c in range(fields):
-            value = control[c] * projected if k >= ahead else weight[k * fields + c] * received
-            tile = jnp.where(line == c, jnp.sum(fold(value), axis=0, keepdims=True), tile)
-        out[8 * k : 8 * k + 8] = tile * ((2.0 if k >= ahead else -2.0) * overlap)
+            tile = jnp.where(line == c, jnp.sum(fold(control[c] * projected), axis=0, keepdims=True), tile)
+        out[8 * k : 8 * k + 8] = tile * (2.0 * overlap)
     out[8 * count : 8 * count + 8] = jnp.where((lane == 0) & (line == 0), overlap * overlap, 0.0)
 
 
@@ -315,23 +293,25 @@
     base, control = call(
         generator_kernel,
         [square, (fields,) + square],
-        [SMEM] * 2 + [HBM] * 4,
+        [HBM] * 6,
         "generators",
         flops=2 * product,
         scratch=[
+            pltpu.SMEM((1, 1), F32),
+            pltpu.SMEM(pattern.shape, jnp.int32),
             pltpu.VMEM((1, states), F32),
             pltpu.VMEM(square, F32),
             pltpu.VMEM(square, F32),
             pltpu.VMEM((fields,) + square, F32),
             pltpu.VMEM(square, F32),
-            pltpu.SemaphoreType.DMA((3 + fields,)),
+            pltpu.SemaphoreType.DMA((5 + fields,)),
         ],
         room=60,
-    )(b1_scale, pattern, relax.reshape(1, states), drift_raw, member_drift[0], control_raw[0])
+    )(b1_scale.reshape(1, 1), pattern, relax.reshape(1, states), drift_raw, member_drift[0], control_raw[0])
     step, pair, local, held = call(
         step_kernel,
         [(count,) + square, (halves,) + square, (max(halves - 1, 1),) + square, square],
-        [SMEM, VMEM, VMEM],
+        [VMEM] * 3,
         "steps",
         flops=50 * product,
         room=32,
@@ -374,23 +354,14 @@
             held = call(
                 functools.partial(join_kernel, functools.partial(digit, r)), square, [VMEM] * 2, "join", flops=product
             )(held, other)
-    ahead = min(AHEAD, count)
-    direct = count - ahead
-    shapes = [(fields * ahead,) + square, square]
-    if direct:
-        shapes += [
-            pltpu.VMEM((direct * states, 3 * states), BF16),
-            pltpu.VMEM((direct, 3 * states, states), BF16),
-        ]
     weights = call(
         functools.partial(sides_kernel, functools.partial(digit, bits - 1)),
-        shapes,
-        [VMEM] * 6,
+        [square, pltpu.VMEM((count * states, 3 * states), BF16), pltpu.VMEM((count, 3 * states, states), BF16)],
+        [VMEM] * 5,
         "sides",
-        flops=20 * product,
-        scratch=[pltpu.VMEM(square, F32)] * 2 + [pltpu.VMEM((fields * states, 3 * states), BF16)],
-        room=20,
-    )(target, after, before, suffix, prefix, control)
+        flops=7 * product,
+        scratch=[pltpu.VMEM(square, F32)] * 2,
+    )(target, after, before, suffix, prefix)
     mine = call(
         gradient_kernel, (8 * count + 8, 128), [VMEM] * (2 + len(weights)), "gradient", flops=3 * product
     )(other, control, *weights)

time: 53.5 us -> 52.1 us (0.974); the launches traced: 52.7 us -> 52 us
  Pallas kernels: 22.3 us -> 19.2 us
  waiting for transfers between devices: 19.2 us -> 21.6 us
    pallas_call x1, Pallas kernels: 4.5 us -> 2.19 us  [per_device(): call(functools.partial(sides_kernel, functools.partial(digit, bits - 1)),...]
    ppermute x4, waiting for transfers between devices: 14.2 us -> 15.9 us  [per_device(): other = lax.ppermute(held, both, pairs)]
    ppermute x1, starting transfers between devices: 2.68 us -> 1.92 us  [per_device(): mine = lax.ppermute(mine, both, home)]
    ppermute x1, waiting for transfers between devices: 3.73 us -> 4.48 us  [per_device(): mine = lax.ppermute(mine, both, home)]
    ppermute x4, starting transfers between devices: 1.97 us -> 2.63 us  [per_device(): other = lax.ppermute(held, both, pairs)]
    pallas_call x1, Pallas kernels: 2.47 us -> 1.82 us  [per_device(): call(generator_kernel, [square, (fields,) + square], [HBM] * 6, 'generato...]
  transfers between devices with their start and end apart: 7 -> 7, of which waited for: 6 -> 6; matrix products, arithmetic and copies ran while one was open for 0% -> 0% of each run, Pallas kernels for 18% -> 13%
where the time goes in v5:
time: 52.1 us; the launch traced here: 52 us
  waiting for transfers between devices  21.6 us (41%)
  Pallas kernels  19.2 us (37%)
  starting transfers between devices  9.78 us (19%)
  between operations  1.4 us (3%)
    ppermute x4, waiting for transfers between devices, per_device(): other = lax.ppermute(held, both, pairs)  15.9 us
    pallas_call x1, Pallas kernels, per_device(): call(step_kernel, [(count,) + square, (halves,) + square, (max(halves - 1...  8.72 us
    ppermute x1, starting transfers between devices, per_device(): lax.ppermute(amplitude, both, [(flat(turned(p, e), e), flat(p, e)) for p...  5.23 us
    ppermute x1, waiting for transfers between devices, per_device(): mine = lax.ppermute(mine, both, home)  4.48 us
    ppermute x4, starting transfers between devices, per_device(): other = lax.ppermute(held, both, pairs)  2.63 us
    pallas_call x1, Pallas kernels, per_device(): call(functools.partial(sides_kernel, functools.partial(digit, bits - 1)),...  2.19 us
    pallas_call x1, Pallas kernels, per_device(): call(gradient_kernel, (8 * count + 8, 128), [VMEM] * (2 + len(weights)),...  2.01 us
    ppermute x1, starting transfers between devices, per_device(): mine = lax.ppermute(mine, both, home)  1.92 us
  transfers between devices with their start and end apart: 7, of which 6 were waited for; matrix products, arithmetic and copies ran while one was open for 0% of the time, Pallas kernels for 13%

profile of v5, /device:TPU:7, one launch (start us, length us, event | category | flops | bytes accessed | tf_op | source)
XLA Modules:
  0.0 52.0 jit_solution(2769570015606119536)
XLA Ops:
  0.6 5.2 %collective-permute-start = (f32[4,6]{1,0:T(4,128)}, f32[4,6]{1,0:T(4,128)S(1)}, u32[]{:S(2)}, u32[]{:S(2)}) collective-permute-start(f32[4,6]{1,0:T(4,128)} %param.13), channel_id=1, source_target_pairs={{0,0},{25,1},{2,2},{17,3},{4,4},{9,5},{6,6},{1,7},{8,8},{27,9},{10... | collective-permute-start | bytes 296 | tf_op jit(solution)/shard_map/ppermute | solution.py:288
  6.5 1.8 %generators.1 = (f32[256,256]{1,0:T(8,128)S(1)}, f32[4,256,256]{2,1,0:T(8,128)S(1)}) custom-call(f32[1,1]{1,0:T(1,128)} %bitcast.5.strength_raw, s32[4,4]{1,0:T(4,128)} %pattern_raw.1, f32[1,256]{1,0:T(1,128)} %bitcast.8, f32[256,256]{1,0:T(8,128)} %drift_raw.1, f32[256,256]{1,0:T(8,128)} %bitcast.7, f32[4,256,256]{2,1,0:T(8,128)} %bitcast.6), custom_call_target="tpu_custom_call" | custom-call | flops 402653184 | bytes 1048576 | tf_op jit(solution)/shard_map/generators/pallas_call | solution.py:293
  8.3 0.0 collective-permute-done.amplitude
  8.4 8.7 %steps.1 = (f32[6,256,256]{2,1,0:T(8,128)S(1)}, f32[3,256,256]{2,1,0:T(8,128)S(1)}, f32[2,256,256]{2,1,0:T(8,128)S(1)}, f32[256,256]{1,0:T(8,128)S(1)}) custom-call(f32[4,6]{1,0:T(4,128)S(1)} %collective-permute-done.amplitude, f32[256,256]{1,0:T(8,128)S(1)} %get-tuple-element.25.base, f32[4,256,256]{2,1,0:T(8,128)S(1)} %get-tuple-element.26.control), custom_call_target="tpu_custom_call" | custom-call | flops 10066329600 | bytes 1048576 | tf_op jit(solution)/shard_map/steps/pallas_call | solution.py:311
  17.1 0.3 collective-permute-start.1
  17.4 1.8 %local.1 = (f32[6,256,256]{2,1,0:T(8,128)S(1)}, f32[6,256,256]{2,1,0:T(8,128)S(1)}) custom-call(f32[6,256,256]{2,1,0:T(8,128)S(1)} %get-tuple-element.28.step, f32[3,256,256]{2,1,0:T(8,128)S(1)} %get-tuple-element.29.pair, f32[2,256,256]{2,1,0:T(8,128)S(1)} %get-tuple-element.30.before, f32[256,256]{1,0:T(8,128)S(1)} %get-tuple-element.27.segment.held), custom_call_target="tpu_custom_call" | custom-call | flops 1006632960 | bytes 1048576 | tf_op jit(solution)/shard_map/local/pallas_call | solution.py:332
  19.2 3.2 %collective-permute-done.1.other.first = f32[256,256]{1,0:T(8,128)S(1)} collective-permute-done((f32[256,256]{1,0:T(8,128)S(1)}, f32[256,256]{1,0:T(8,128)S(1)}, u32[]{:S(2)}, u32[]{:S(2)}) %collective-permute-start.1) | collective-permute-done | bytes 262176 | tf_op jit(solution)/shard_map/ppermute | solution.py:330
  22.4 0.4 join.3.held
  22.8 0.0 copy-start
  22.8 2.0 %collective-permute-start.2 = (f32[256,256]{1,0:T(8,128)S(1)}, f32[256,256]{1,0:T(8,128)S(1)}, u32[]{:S(2)}, u32[]{:S(2)}) collective-permute-start(f32[256,256]{1,0:T(8,128)S(1)} %join.3.held), channel_id=1, source_target_pairs={{0,4},{2,6},{4,0},{6,2},{8,12},{10,14},{12,8},{14,10},{16,20},{18,... | collective-permute-start | bytes 786440 | tf_op jit(solution)/shard_map/ppermute | solution.py:330
  24.8 5.2 %collective-permute-done.2.other = f32[256,256]{1,0:T(8,128)S(1)} collective-permute-done((f32[256,256]{1,0:T(8,128)S(1)}, f32[256,256]{1,0:T(8,128)S(1)}, u32[]{:S(2)}, u32[]{:S(2)}) %collective-permute-start.2) | collective-permute-done | bytes 262176 | tf_op jit(solution)/shard_map/ppermute | solution.py:330
  30.0 0.4 join.4.held
  30.4 0.2 collective-permute-start.3
  30.6 0.4 reach_first.1
  31.0 4.6 %collective-permute-done.3.other = f32[256,256]{1,0:T(8,128)S(1)} collective-permute-done((f32[256,256]{1,0:T(8,128)S(1)}, f32[256,256]{1,0:T(8,128)S(1)}, u32[]{:S(2)}, u32[]{:S(2)}) %collective-permute-start.3) | collective-permute-done | bytes 262176 | tf_op jit(solution)/shard_map/ppermute | solution.py:330
  35.7 0.4 join.5
  36.1 0.1 collective-permute-start.4
  36.2 0.4 reach.1
  36.6 0.0 copy-done
  36.6 2.2 %sides.1 = (f32[256,256]{1,0:T(8,128)S(1)}, bf16[1536,768]{1,0:T(8,128)(2,1)S(1)}, bf16[6,768,256]{2,1,0:T(8,128)(2,1)S(1)}) custom-call(f32[256,256]{1,0:T(8,128)S(1)} %copy-done, f32[256,256]{1,0:T(8,128)S(1)} %get-tuple-element.39.after, f32[256,256]{1,0:T(8,128)S(1)} %get-tuple-element.40.before, f32[6,256,256]{2,1,0:T(8,128)S(1)} %get-tuple-element.41.suffix, ...), custom_call_target="tpu_custom_call" | custom-call | flops 1409286144 | bytes 1048576 | tf_op jit(solution)/shard_map/sides/pallas_call | solution.py:357
  38.8 2.9 %collective-permute-done.4.other = f32[256,256]{1,0:T(8,128)S(1)} collective-permute-done((f32[256,256]{1,0:T(8,128)S(1)}, f32[256,256]{1,0:T(8,128)S(1)}, u32[]{:S(2)}, u32[]{:S(2)}) %collective-permute-start.4) | collective-permute-done | bytes 262176 | tf_op jit(solution)/shard_map/ppermute | solution.py:330
  41.7 2.0 %gradient.1 = f32[56,128]{1,0:T(8,128)S(1)} custom-call(f32[256,256]{1,0:T(8,128)S(1)} %collective-permute-done.4.other, f32[4,256,256]{2,1,0:T(8,128)S(1)} %get-tuple-element.26.control, f32[256,256]{1,0:T(8,128)S(1)} %get-tuple-element.43.overlap_weight, bf16[1536,768]{1,0:T(8,128)(2,1)S(1)} %get-tuple-element.44.left, ...), custom_call_target="tpu_custom_call" | custom-call | flops 603979776 | bytes 1048576 | tf_op jit(solution)/shard_map/gradient/pallas_call | solution.py:365
  43.7 1.9 %collective-permute-start.5 = (f32[56,128]{1,0:T(8,128)S(1)}, f32[56,128]{1,0:T(8,128)S(1)}, u32[]{:S(2)}, u32[]{:S(2)}) collective-permute-start(f32[56,128]{1,0:T(8,128)S(1)} %gradient.1), channel_id=1, source_target_pairs={{0,0},{1,25},{2,2},{3,17},{4,4},{5,9},{6,6},{7,1},{8,8},{9,27},{10... | collective-permute-start | bytes 86024 | tf_op jit(solution)/shard_map/ppermute | solution.py:370
  45.6 4.5 %collective-permute-done.5.first = f32[56,128]{1,0:T(8,128)S(1)} collective-permute-done((f32[56,128]{1,0:T(8,128)S(1)}, f32[56,128]{1,0:T(8,128)S(1)}, u32[]{:S(2)}, u32[]{:S(2)}) %collective-permute-start.5) | collective-permute-done | bytes 28704 | tf_op jit(solution)/shard_map/ppermute | solution.py:370
  50.1 0.0 collective-permute-start.6
  50.1 1.2 %collective-permute-done.6.second = f32[56,128]{1,0:T(8,128)S(1)} collective-permute-done((f32[56,128]{1,0:T(8,128)S(1)}, f32[56,128]{1,0:T(8,128)S(1)}, u32[]{:S(2)}, u32[]{:S(2)}) %collective-permute-start.6) | collective-permute-done | bytes 28704 | tf_op jit(solution)/shard_map/ppermute | solution.py:371
  51.3 0.7 %finish.1 = (f32[4,6]{1,0:T(4,128)}, f32[1,1]{1,0:T(1,128)}) custom-call(f32[56,128]{1,0:T(8,128)S(1)} %collective-permute-done.5.first, f32[56,128]{1,0:T(8,128)S(1)} %collective-permute-done.6.second), custom_call_target="tpu_custom_call" | custom-call | tf_op jit(solution)/shard_map/finish/pallas_call | solution.py:374
Async XLA Ops:
  0.6 7.7 %collective-permute-start = (f32[4,6]{1,0:T(4,128)}, f32[4,6]{1,0:T(4,128)S(1)}, u32[]{:S(2)}, u32[]{:S(2)}) collective-permute-start(f32[4,6]{1,0:T(4,128)} %param.13), channel_id=1, source_target_pairs={{0,0},{25,1},{2,2},{17,3},{4,4},{9,5},{6,6},{1,7},{8,8},{27,9},{10... | collective-permute-start | bytes 296 | tf_op jit(solution)/shard_map/ppermute | solution.py:288
  17.1 5.3 %collective-permute-start.1 = (f32[256,256]{1,0:T(8,128)S(1)}, f32[256,256]{1,0:T(8,128)S(1)}, u32[]{:S(2)}, u32[]{:S(2)}) collective-permute-start(f32[256,256]{1,0:T(8,128)S(1)} %get-tuple-element.27.segment.held), channel_id=1, source_target_pairs={{0,2},{2,0},{4,6},{6,4},{8,10},{10,8},{12,14},{14,12},{16,18},{18,... | collective-permute-start | bytes 786440 | tf_op jit(solution)/shard_map/ppermute | solution.py:330
  22.8 13.8 %copy-start = (f32[256,256]{1,0:T(8,128)S(1)}, f32[256,256]{1,0:T(8,128)}, u32[]{:S(2)}) copy-start(f32[256,256]{1,0:T(8,128)} %target.1) | copy-start | bytes 786436
  22.8 7.2 %collective-permute-start.2 = (f32[256,256]{1,0:T(8,128)S(1)}, f32[256,256]{1,0:T(8,128)S(1)}, u32[]{:S(2)}, u32[]{:S(2)}) collective-permute-start(f32[256,256]{1,0:T(8,128)S(1)} %join.3.held), channel_id=1, source_target_pairs={{0,4},{2,6},{4,0},{6,2},{8,12},{10,14},{12,8},{14,10},{16,20},{18,... | collective-permute-start | bytes 786440 | tf_op jit(solution)/shard_map/ppermute | solution.py:330
  30.4 5.3 %collective-permute-start.3 = (f32[256,256]{1,0:T(8,128)S(1)}, f32[256,256]{1,0:T(8,128)S(1)}, u32[]{:S(2)}, u32[]{:S(2)}) collective-permute-start(f32[256,256]{1,0:T(8,128)S(1)} %join.4.held), channel_id=1, source_target_pairs={{0,8},{2,10},{4,12},{6,14},{8,0},{10,2},{12,4},{14,6},{16,24},{18,... | collective-permute-start | bytes 786440 | tf_op jit(solution)/shard_map/ppermute | solution.py:330
  36.1 5.6 %collective-permute-start.4 = (f32[256,256]{1,0:T(8,128)S(1)}, f32[256,256]{1,0:T(8,128)S(1)}, u32[]{:S(2)}, u32[]{:S(2)}) collective-permute-start(f32[256,256]{1,0:T(8,128)S(1)} %join.5), channel_id=1, source_target_pairs={{0,24},{2,26},{4,28},{6,30},{8,16},{10,18},{12,20},{14,22},{16,8},... | collective-permute-start | bytes 786440 | tf_op jit(solution)/shard_map/ppermute | solution.py:330
  43.7 6.4 %collective-permute-start.5 = (f32[56,128]{1,0:T(8,128)S(1)}, f32[56,128]{1,0:T(8,128)S(1)}, u32[]{:S(2)}, u32[]{:S(2)}) collective-permute-start(f32[56,128]{1,0:T(8,128)S(1)} %gradient.1), channel_id=1, source_target_pairs={{0,0},{1,25},{2,2},{3,17},{4,4},{5,9},{6,6},{7,1},{8,8},{9,27},{10... | collective-permute-start | bytes 86024 | tf_op jit(solution)/shard_map/ppermute | solution.py:370
  50.1 1.2 %collective-permute-start.6 = (f32[56,128]{1,0:T(8,128)S(1)}, f32[56,128]{1,0:T(8,128)S(1)}, u32[]{:S(2)}, u32[]{:S(2)}) collective-permute-start(f32[56,128]{1,0:T(8,128)S(1)} %collective-permute-done.5.first), channel_id=1, source_target_pairs={{0,1},{1,0},{2,3},{3,2},{4,5},{5,4},{6,7},{7,6},{8,9},{9,8},{10,11... | collective-permute-start | bytes 86024 | tf_op jit(solution)/shard_map/ppermute | solution.py:371

commit v6 on v5

--- a/solution.py
+++ b/solution.py
@@ -366,9 +366,11 @@
         gradient_kernel, (8 * count + 8, 128), [VMEM] * (2 + len(weights)), "gradient", flops=3 * product
     )(other, control, *weights)
     if turn:
-        home = [(flat(p, e), flat(turned(p, e), e)) for p in range(segments) for e in range(members)]
-        mine = lax.ppermute(mine, both, home)
-        both_terms = (mine, lax.ppermute(mine, "ens", [(0, 1), (1, 0)]))
+        first = [(flat(p, 1), flat(turned(p, 1), 0)) for p in range(segments)]
+        first += [(flat(p, 0), flat(p, 1)) for p in range(segments)]
+        second = [(flat(p, 1), flat(turned(p, 1), 1)) for p in range(segments)]
+        second += [(flat(p, 0), flat(p, 0)) for p in range(segments)]
+        both_terms = (lax.ppermute(mine, both, first), lax.ppermute(mine, both, second))
     else:
         both_terms = (lax.psum(mine, "ens"), jnp.zeros_like(mine))
     gradient, fidelity = pl.pallas_call(

time: 52.1 us -> 51.7 us (level); the launches traced: 52 us -> 50.8 us
  waiting for transfers between devices: 21.6 us -> 20.3 us
    ppermute x2, waiting for transfers between devices: 5.68 us -> 4.42 us  [the longest x1 4.42 us: per_device(): lax.ppermute(mine, both, second)]
  transfers between devices with their start and end apart: 7 -> 7, of which waited for: 6 -> 5; matrix products, arithmetic and copies ran while one was open for 0% -> 0% of each run, Pallas kernels for 13% -> 13%
where the time goes in v6:
time: 51.7 us; the launch traced here: 50.8 us
  waiting for transfers between devices  20.3 us (39%)
  Pallas kernels  19.2 us (37%)
  starting transfers between devices  9.83 us (19%)
  between operations  1.4 us (3%)
    ppermute x4, waiting for transfers between devices, per_device(): other = lax.ppermute(held, both, pairs)  15.9 us
    pallas_call x1, Pallas kernels, per_device(): call(step_kernel, [(count,) + square, (halves,) + square, (max(halves - 1...  8.72 us
    ppermute x1, starting transfers between devices, per_device(): lax.ppermute(amplitude, both, [(flat(turned(p, e), e), flat(p, e)) for p...  5.23 us
    ppermute x1, waiting for transfers between devices, per_device(): lax.ppermute(mine, both, second)  4.42 us
    ppermute x4, starting transfers between devices, per_device(): other = lax.ppermute(held, both, pairs)  2.63 us
    pallas_call x1, Pallas kernels, per_device(): call(functools.partial(sides_kernel, functools.partial(digit, bits - 1)),...  2.19 us
    pallas_call x1, Pallas kernels, per_device(): call(gradient_kernel, (8 * count + 8, 128), [VMEM] * (2 + len(weights)),...  2.01 us
    ppermute x1, starting transfers between devices, per_device(): lax.ppermute(mine, both, second)  1.92 us
  transfers between devices with their start and end apart: 7, of which 5 were waited for; matrix products, arithmetic and copies ran while one was open for 0% of the time, Pallas kernels for 13%

profile of v6, /device:TPU:7, one launch (start us, length us, event | category | flops | bytes accessed | tf_op | source)
XLA Modules:
  0.0 50.8 jit_solution(10346500104262034945)
XLA Ops:
  0.6 5.2 %collective-permute-start = (f32[4,6]{1,0:T(4,128)}, f32[4,6]{1,0:T(4,128)S(1)}, u32[]{:S(2)}, u32[]{:S(2)}) collective-permute-start(f32[4,6]{1,0:T(4,128)} %param.13), channel_id=1, source_target_pairs={{0,0},{25,1},{2,2},{17,3},{4,4},{9,5},{6,6},{1,7},{8,8},{27,9},{10... | collective-permute-start | bytes 296 | tf_op jit(solution)/shard_map/ppermute | solution.py:288
  6.5 1.8 %generators.1 = (f32[256,256]{1,0:T(8,128)S(1)}, f32[4,256,256]{2,1,0:T(8,128)S(1)}) custom-call(f32[1,1]{1,0:T(1,128)} %bitcast.5.strength_raw, s32[4,4]{1,0:T(4,128)} %pattern_raw.1, f32[1,256]{1,0:T(1,128)} %bitcast.8, f32[256,256]{1,0:T(8,128)} %drift_raw.1, f32[256,256]{1,0:T(8,128)} %bitcast.7, f32[4,256,256]{2,1,0:T(8,128)} %bitcast.6), custom_call_target="tpu_custom_call" | custom-call | flops 402653184 | bytes 1048576 | tf_op jit(solution)/shard_map/generators/pallas_call | solution.py:293
  8.3 0.0 collective-permute-done.amplitude
  8.4 8.7 %steps.1 = (f32[6,256,256]{2,1,0:T(8,128)S(1)}, f32[3,256,256]{2,1,0:T(8,128)S(1)}, f32[2,256,256]{2,1,0:T(8,128)S(1)}, f32[256,256]{1,0:T(8,128)S(1)}) custom-call(f32[4,6]{1,0:T(4,128)S(1)} %collective-permute-done.amplitude, f32[256,256]{1,0:T(8,128)S(1)} %get-tuple-element.25.base, f32[4,256,256]{2,1,0:T(8,128)S(1)} %get-tuple-element.26.control), custom_call_target="tpu_custom_call" | custom-call | flops 10066329600 | bytes 1048576 | tf_op jit(solution)/shard_map/steps/pallas_call | solution.py:311
  17.1 0.3 collective-permute-start.1
  17.4 1.8 %local.1 = (f32[6,256,256]{2,1,0:T(8,128)S(1)}, f32[6,256,256]{2,1,0:T(8,128)S(1)}) custom-call(f32[6,256,256]{2,1,0:T(8,128)S(1)} %get-tuple-element.28.step, f32[3,256,256]{2,1,0:T(8,128)S(1)} %get-tuple-element.29.pair, f32[2,256,256]{2,1,0:T(8,128)S(1)} %get-tuple-element.30.before, f32[256,256]{1,0:T(8,128)S(1)} %get-tuple-element.27.segment.held), custom_call_target="tpu_custom_call" | custom-call | flops 1006632960 | bytes 1048576 | tf_op jit(solution)/shard_map/local/pallas_call | solution.py:332
  19.2 3.2 %collective-permute-done.1.other.first = f32[256,256]{1,0:T(8,128)S(1)} collective-permute-done((f32[256,256]{1,0:T(8,128)S(1)}, f32[256,256]{1,0:T(8,128)S(1)}, u32[]{:S(2)}, u32[]{:S(2)}) %collective-permute-start.1) | collective-permute-done | bytes 262176 | tf_op jit(solution)/shard_map/ppermute | solution.py:330
  22.4 0.4 join.3.held
  22.8 0.0 copy-start
  22.8 2.0 %collective-permute-start.2 = (f32[256,256]{1,0:T(8,128)S(1)}, f32[256,256]{1,0:T(8,128)S(1)}, u32[]{:S(2)}, u32[]{:S(2)}) collective-permute-start(f32[256,256]{1,0:T(8,128)S(1)} %join.3.held), channel_id=1, source_target_pairs={{0,4},{2,6},{4,0},{6,2},{8,12},{10,14},{12,8},{14,10},{16,20},{18,... | collective-permute-start | bytes 786440 | tf_op jit(solution)/shard_map/ppermute | solution.py:330
  24.8 5.2 %collective-permute-done.2.other = f32[256,256]{1,0:T(8,128)S(1)} collective-permute-done((f32[256,256]{1,0:T(8,128)S(1)}, f32[256,256]{1,0:T(8,128)S(1)}, u32[]{:S(2)}, u32[]{:S(2)}) %collective-permute-start.2) | collective-permute-done | bytes 262176 | tf_op jit(solution)/shard_map/ppermute | solution.py:330
  30.0 0.4 join.4.held
  30.4 0.2 collective-permute-start.3
  30.6 0.4 reach_first.1
  31.0 4.6 %collective-permute-done.3.other = f32[256,256]{1,0:T(8,128)S(1)} collective-permute-done((f32[256,256]{1,0:T(8,128)S(1)}, f32[256,256]{1,0:T(8,128)S(1)}, u32[]{:S(2)}, u32[]{:S(2)}) %collective-permute-start.3) | collective-permute-done | bytes 262176 | tf_op jit(solution)/shard_map/ppermute | solution.py:330
  35.7 0.4 join.5
  36.1 0.1 collective-permute-start.4
  36.2 0.4 reach.1
  36.6 0.0 copy-done
  36.6 2.2 %sides.1 = (f32[256,256]{1,0:T(8,128)S(1)}, bf16[1536,768]{1,0:T(8,128)(2,1)S(1)}, bf16[6,768,256]{2,1,0:T(8,128)(2,1)S(1)}) custom-call(f32[256,256]{1,0:T(8,128)S(1)} %copy-done, f32[256,256]{1,0:T(8,128)S(1)} %get-tuple-element.39.after, f32[256,256]{1,0:T(8,128)S(1)} %get-tuple-element.40.before, f32[6,256,256]{2,1,0:T(8,128)S(1)} %get-tuple-element.41.suffix, ...), custom_call_target="tpu_custom_call" | custom-call | flops 1409286144 | bytes 1048576 | tf_op jit(solution)/shard_map/sides/pallas_call | solution.py:357
  38.8 2.9 %collective-permute-done.4.other = f32[256,256]{1,0:T(8,128)S(1)} collective-permute-done((f32[256,256]{1,0:T(8,128)S(1)}, f32[256,256]{1,0:T(8,128)S(1)}, u32[]{:S(2)}, u32[]{:S(2)}) %collective-permute-start.4) | collective-permute-done | bytes 262176 | tf_op jit(solution)/shard_map/ppermute | solution.py:330
  41.7 2.0 %gradient.1 = f32[56,128]{1,0:T(8,128)S(1)} custom-call(f32[256,256]{1,0:T(8,128)S(1)} %collective-permute-done.4.other, f32[4,256,256]{2,1,0:T(8,128)S(1)} %get-tuple-element.26.control, f32[256,256]{1,0:T(8,128)S(1)} %get-tuple-element.43.overlap_weight, bf16[1536,768]{1,0:T(8,128)(2,1)S(1)} %get-tuple-element.44.left, ...), custom_call_target="tpu_custom_call" | custom-call | flops 603979776 | bytes 1048576 | tf_op jit(solution)/shard_map/gradient/pallas_call | solution.py:365
  43.7 1.9 %collective-permute-start.6 = (f32[56,128]{1,0:T(8,128)S(1)}, f32[56,128]{1,0:T(8,128)S(1)}, u32[]{:S(2)}, u32[]{:S(2)}) collective-permute-start(f32[56,128]{1,0:T(8,128)S(1)} %gradient.1), channel_id=1, source_target_pairs={{1,25},{3,17},{5,9},{7,1},{9,27},{11,19},{13,11},{15,3},{17,29},{1... | collective-permute-start | bytes 86024 | tf_op jit(solution)/shard_map/ppermute | solution.py:373
  45.6 0.1 collective-permute-start.5
  45.7 4.4 %collective-permute-done.6.second = f32[56,128]{1,0:T(8,128)S(1)} collective-permute-done((f32[56,128]{1,0:T(8,128)S(1)}, f32[56,128]{1,0:T(8,128)S(1)}, u32[]{:S(2)}, u32[]{:S(2)}) %collective-permute-start.6) | collective-permute-done | bytes 28704 | tf_op jit(solution)/shard_map/ppermute | solution.py:373
  50.1 0.0 collective-permute-done.5.first
  50.1 0.7 %finish.1 = (f32[4,6]{1,0:T(4,128)}, f32[1,1]{1,0:T(1,128)}) custom-call(f32[56,128]{1,0:T(8,128)S(1)} %collective-permute-done.5.first, f32[56,128]{1,0:T(8,128)S(1)} %collective-permute-done.6.second), custom_call_target="tpu_custom_call" | custom-call | tf_op jit(solution)/shard_map/finish/pallas_call | solution.py:376
Async XLA Ops:
  0.6 7.7 %collective-permute-start = (f32[4,6]{1,0:T(4,128)}, f32[4,6]{1,0:T(4,128)S(1)}, u32[]{:S(2)}, u32[]{:S(2)}) collective-permute-start(f32[4,6]{1,0:T(4,128)} %param.13), channel_id=1, source_target_pairs={{0,0},{25,1},{2,2},{17,3},{4,4},{9,5},{6,6},{1,7},{8,8},{27,9},{10... | collective-permute-start | bytes 296 | tf_op jit(solution)/shard_map/ppermute | solution.py:288
  17.1 5.3 %collective-permute-start.1 = (f32[256,256]{1,0:T(8,128)S(1)}, f32[256,256]{1,0:T(8,128)S(1)}, u32[]{:S(2)}, u32[]{:S(2)}) collective-permute-start(f32[256,256]{1,0:T(8,128)S(1)} %get-tuple-element.27.segment.held), channel_id=1, source_target_pairs={{0,2},{2,0},{4,6},{6,4},{8,10},{10,8},{12,14},{14,12},{16,18},{18,... | collective-permute-start | bytes 786440 | tf_op jit(solution)/shard_map/ppermute | solution.py:330
  22.8 13.8 %copy-start = (f32[256,256]{1,0:T(8,128)S(1)}, f32[256,256]{1,0:T(8,128)}, u32[]{:S(2)}) copy-start(f32[256,256]{1,0:T(8,128)} %target.1) | copy-start | bytes 786436
  22.8 7.2 %collective-permute-start.2 = (f32[256,256]{1,0:T(8,128)S(1)}, f32[256,256]{1,0:T(8,128)S(1)}, u32[]{:S(2)}, u32[]{:S(2)}) collective-permute-start(f32[256,256]{1,0:T(8,128)S(1)} %join.3.held), channel_id=1, source_target_pairs={{0,4},{2,6},{4,0},{6,2},{8,12},{10,14},{12,8},{14,10},{16,20},{18,... | collective-permute-start | bytes 786440 | tf_op jit(solution)/shard_map/ppermute | solution.py:330
  30.4 5.3 %collective-permute-start.3 = (f32[256,256]{1,0:T(8,128)S(1)}, f32[256,256]{1,0:T(8,128)S(1)}, u32[]{:S(2)}, u32[]{:S(2)}) collective-permute-start(f32[256,256]{1,0:T(8,128)S(1)} %join.4.held), channel_id=1, source_target_pairs={{0,8},{2,10},{4,12},{6,14},{8,0},{10,2},{12,4},{14,6},{16,24},{18,... | collective-permute-start | bytes 786440 | tf_op jit(solution)/shard_map/ppermute | solution.py:330
  36.1 5.6 %collective-permute-start.4 = (f32[256,256]{1,0:T(8,128)S(1)}, f32[256,256]{1,0:T(8,128)S(1)}, u32[]{:S(2)}, u32[]{:S(2)}) collective-permute-start(f32[256,256]{1,0:T(8,128)S(1)} %join.5), channel_id=1, source_target_pairs={{0,24},{2,26},{4,28},{6,30},{8,16},{10,18},{12,20},{14,22},{16,8},... | collective-permute-start | bytes 786440 | tf_op jit(solution)/shard_map/ppermute | solution.py:330
  43.7 6.4 %collective-permute-start.6 = (f32[56,128]{1,0:T(8,128)S(1)}, f32[56,128]{1,0:T(8,128)S(1)}, u32[]{:S(2)}, u32[]{:S(2)}) collective-permute-start(f32[56,128]{1,0:T(8,128)S(1)} %gradient.1), channel_id=1, source_target_pairs={{1,25},{3,17},{5,9},{7,1},{9,27},{11,19},{13,11},{15,3},{17,29},{1... | collective-permute-start | bytes 86024 | tf_op jit(solution)/shard_map/ppermute | solution.py:373
  45.6 4.5 %collective-permute-start.5 = (f32[56,128]{1,0:T(8,128)S(1)}, f32[56,128]{1,0:T(8,128)S(1)}, u32[]{:S(2)}, u32[]{:S(2)}) collective-permute-start(f32[56,128]{1,0:T(8,128)S(1)} %gradient.1), channel_id=1, source_target_pairs={{1,24},{3,16},{5,8},{7,0},{9,26},{11,18},{13,10},{15,2},{17,28},{1... | collective-permute-start | bytes 86024 | tf_op jit(solution)/shard_map/ppermute | solution.py:373

commit v7 on v6

--- a/solution.py
+++ b/solution.py
@@ -45,7 +45,11 @@
 def three(first, second, dims=NN):
     a1, a2 = parts(first, 2)
     b1, b2 = parts(second, 2)
-    return dot(a1, b1, dims) + (dot(a1, b2, dims) + dot(a2, b1, dims))
+    if dims == TN:
+        return dot(a1, b1, dims) + (dot(a1, b2, dims) + dot(a2, b1, dims))
+    rows = first.shape[0]
+    large = dot(jnp.concatenate([a1, a2], axis=0), b1, dims)
+    return large[:rows] + (dot(a1, b2, dims) + large[rows:])
 
 
 def unit(states):
@@ -215,10 +219,9 @@
 
     received = other[...]
     overlap = jnp.sum(fold(overlap_weight[...] * received))
-    received_parts = along(received, 1, SECOND)
+    middle = dot(left[...], along(received, 1, SECOND), NT)
     for k in range(count):
-        middle = dot(left[k * states : (k + 1) * states], received_parts, NT)
-        projected = dot(along(middle, 1, FIRST), right[k])
+        projected = dot(along(middle[k * states : (k + 1) * states], 1, FIRST), right[k])
         tile = jnp.zeros((8, lanes), F32)
         for c in range(fields):
             tile = jnp.where(line == c, jnp.sum(fold(control[c] * projected), axis=0, keepdims=True), tile)

time: 51.7 us -> 52.1 us (level)
  no operation moved by 1% of the time
where the time goes in v7:
time: 52.1 us; the launch traced here: 51.2 us
  waiting for transfers between devices  20.3 us (39%)
  Pallas kernels  19.6 us (38%)
  starting transfers between devices  9.84 us (19%)
  between operations  1.41 us (3%)
    ppermute x4, waiting for transfers between devices, per_device(): other = lax.ppermute(held, both, pairs)  15.9 us
    pallas_call x1, Pallas kernels, per_device(): call(step_kernel, [(count,) + square, (halves,) + square, (max(halves - 1...  8.72 us
    ppermute x1, starting transfers between devices, per_device(): lax.ppermute(amplitude, both, [(flat(turned(p, e), e), flat(p, e)) for p...  5.23 us
    ppermute x1, waiting for transfers between devices, per_device(): lax.ppermute(mine, both, second)  4.42 us
    ppermute x4, starting transfers between devices, per_device(): other = lax.ppermute(held, both, pairs)  2.63 us
    pallas_call x1, Pallas kernels, per_device(): call(gradient_kernel, (8 * count + 8, 128), [VMEM] * (2 + len(weights)),...  2.48 us
    pallas_call x1, Pallas kernels, per_device(): call(functools.partial(sides_kernel, functools.partial(digit, bits - 1)),...  2.19 us
    ppermute x1, starting transfers between devices, per_device(): lax.ppermute(mine, both, second)  1.92 us
  transfers between devices with their start and end apart: 7, of which 5 were waited for; matrix products, arithmetic and copies ran while one was open for 0% of the time, Pallas kernels for 13%

profile of v7, /device:TPU:7, one launch (start us, length us, event | category | flops | bytes accessed | tf_op | source)
XLA Modules:
  0.0 51.2 jit_solution(17449426072469385802)
XLA Ops:
  0.6 5.2 %collective-permute-start = (f32[4,6]{1,0:T(4,128)}, f32[4,6]{1,0:T(4,128)S(1)}, u32[]{:S(2)}, u32[]{:S(2)}) collective-permute-start(f32[4,6]{1,0:T(4,128)} %param.13), channel_id=1, source_target_pairs={{0,0},{25,1},{2,2},{17,3},{4,4},{9,5},{6,6},{1,7},{8,8},{27,9},{10... | collective-permute-start | bytes 296 | tf_op jit(solution)/shard_map/ppermute | solution.py:291
  6.5 1.8 %generators.1 = (f32[256,256]{1,0:T(8,128)S(1)}, f32[4,256,256]{2,1,0:T(8,128)S(1)}) custom-call(f32[1,1]{1,0:T(1,128)} %bitcast.5.strength_raw, s32[4,4]{1,0:T(4,128)} %pattern_raw.1, f32[1,256]{1,0:T(1,128)} %bitcast.8, f32[256,256]{1,0:T(8,128)} %drift_raw.1, f32[256,256]{1,0:T(8,128)} %bitcast.7, f32[4,256,256]{2,1,0:T(8,128)} %bitcast.6), custom_call_target="tpu_custom_call" | custom-call | flops 402653184 | bytes 1048576 | tf_op jit(solution)/shard_map/generators/pallas_call | solution.py:296
  8.3 0.0 collective-permute-done.amplitude
  8.4 8.7 %steps.1 = (f32[6,256,256]{2,1,0:T(8,128)S(1)}, f32[3,256,256]{2,1,0:T(8,128)S(1)}, f32[2,256,256]{2,1,0:T(8,128)S(1)}, f32[256,256]{1,0:T(8,128)S(1)}) custom-call(f32[4,6]{1,0:T(4,128)S(1)} %collective-permute-done.amplitude, f32[256,256]{1,0:T(8,128)S(1)} %get-tuple-element.25.base, f32[4,256,256]{2,1,0:T(8,128)S(1)} %get-tuple-element.26.control), custom_call_target="tpu_custom_call" | custom-call | flops 10066329600 | bytes 1048576 | tf_op jit(solution)/shard_map/steps/pallas_call | solution.py:314
  17.1 0.3 collective-permute-start.1
  17.4 1.8 %local.1 = (f32[6,256,256]{2,1,0:T(8,128)S(1)}, f32[6,256,256]{2,1,0:T(8,128)S(1)}) custom-call(f32[6,256,256]{2,1,0:T(8,128)S(1)} %get-tuple-element.28.step, f32[3,256,256]{2,1,0:T(8,128)S(1)} %get-tuple-element.29.pair, f32[2,256,256]{2,1,0:T(8,128)S(1)} %get-tuple-element.30.before, f32[256,256]{1,0:T(8,128)S(1)} %get-tuple-element.27.segment.held), custom_call_target="tpu_custom_call" | custom-call | flops 1006632960 | bytes 1048576 | tf_op jit(solution)/shard_map/local/pallas_call | solution.py:335
  19.2 3.2 %collective-permute-done.1.other.first = f32[256,256]{1,0:T(8,128)S(1)} collective-permute-done((f32[256,256]{1,0:T(8,128)S(1)}, f32[256,256]{1,0:T(8,128)S(1)}, u32[]{:S(2)}, u32[]{:S(2)}) %collective-permute-start.1) | collective-permute-done | bytes 262176 | tf_op jit(solution)/shard_map/ppermute | solution.py:333
  22.4 0.4 join.3.held
  22.8 0.0 copy-start
  22.8 2.0 %collective-permute-start.2 = (f32[256,256]{1,0:T(8,128)S(1)}, f32[256,256]{1,0:T(8,128)S(1)}, u32[]{:S(2)}, u32[]{:S(2)}) collective-permute-start(f32[256,256]{1,0:T(8,128)S(1)} %join.3.held), channel_id=1, source_target_pairs={{0,4},{2,6},{4,0},{6,2},{8,12},{10,14},{12,8},{14,10},{16,20},{18,... | collective-permute-start | bytes 786440 | tf_op jit(solution)/shard_map/ppermute | solution.py:333
  24.8 5.2 %collective-permute-done.2.other = f32[256,256]{1,0:T(8,128)S(1)} collective-permute-done((f32[256,256]{1,0:T(8,128)S(1)}, f32[256,256]{1,0:T(8,128)S(1)}, u32[]{:S(2)}, u32[]{:S(2)}) %collective-permute-start.2) | collective-permute-done | bytes 262176 | tf_op jit(solution)/shard_map/ppermute | solution.py:333
  30.0 0.4 join.4.held
  30.4 0.2 collective-permute-start.3
  30.6 0.4 reach_first.1
  31.0 4.6 %collective-permute-done.3.other = f32[256,256]{1,0:T(8,128)S(1)} collective-permute-done((f32[256,256]{1,0:T(8,128)S(1)}, f32[256,256]{1,0:T(8,128)S(1)}, u32[]{:S(2)}, u32[]{:S(2)}) %collective-permute-start.3) | collective-permute-done | bytes 262176 | tf_op jit(solution)/shard_map/ppermute | solution.py:333
  35.7 0.4 join.5
  36.1 0.1 collective-permute-start.4
  36.2 0.4 reach.1
  36.6 0.0 copy-done
  36.6 2.2 %sides.1 = (f32[256,256]{1,0:T(8,128)S(1)}, bf16[1536,768]{1,0:T(8,128)(2,1)S(1)}, bf16[6,768,256]{2,1,0:T(8,128)(2,1)S(1)}) custom-call(f32[256,256]{1,0:T(8,128)S(1)} %copy-done, f32[256,256]{1,0:T(8,128)S(1)} %get-tuple-element.39.after, f32[256,256]{1,0:T(8,128)S(1)} %get-tuple-element.40.before, f32[6,256,256]{2,1,0:T(8,128)S(1)} %get-tuple-element.41.suffix, ...), custom_call_target="tpu_custom_call" | custom-call | flops 1409286144 | bytes 1048576 | tf_op jit(solution)/shard_map/sides/pallas_call | solution.py:360
  38.8 2.9 %collective-permute-done.4.other = f32[256,256]{1,0:T(8,128)S(1)} collective-permute-done((f32[256,256]{1,0:T(8,128)S(1)}, f32[256,256]{1,0:T(8,128)S(1)}, u32[]{:S(2)}, u32[]{:S(2)}) %collective-permute-start.4) | collective-permute-done | bytes 262176 | tf_op jit(solution)/shard_map/ppermute | solution.py:333
  41.7 2.5 %gradient.1 = f32[56,128]{1,0:T(8,128)S(1)} custom-call(f32[256,256]{1,0:T(8,128)S(1)} %collective-permute-done.4.other, f32[4,256,256]{2,1,0:T(8,128)S(1)} %get-tuple-element.26.control, f32[256,256]{1,0:T(8,128)S(1)} %get-tuple-element.43.overlap_weight, bf16[1536,768]{1,0:T(8,128)(2,1)S(1)} %get-tuple-element.44.left, ...), custom_call_target="tpu_custom_call" | custom-call | flops 603979776 | bytes 1048576 | tf_op jit(solution)/shard_map/gradient/pallas_call | solution.py:368
  44.1 1.9 %collective-permute-start.6 = (f32[56,128]{1,0:T(8,128)S(1)}, f32[56,128]{1,0:T(8,128)S(1)}, u32[]{:S(2)}, u32[]{:S(2)}) collective-permute-start(f32[56,128]{1,0:T(8,128)S(1)} %gradient.1), channel_id=1, source_target_pairs={{1,25},{3,17},{5,9},{7,1},{9,27},{11,19},{13,11},{15,3},{17,29},{1... | collective-permute-start | bytes 86024 | tf_op jit(solution)/shard_map/ppermute | solution.py:376
  46.1 0.1 collective-permute-start.5
  46.1 4.4 %collective-permute-done.6.second = f32[56,128]{1,0:T(8,128)S(1)} collective-permute-done((f32[56,128]{1,0:T(8,128)S(1)}, f32[56,128]{1,0:T(8,128)S(1)}, u32[]{:S(2)}, u32[]{:S(2)}) %collective-permute-start.6) | collective-permute-done | bytes 28704 | tf_op jit(solution)/shard_map/ppermute | solution.py:376
  50.6 0.0 collective-permute-done.5.first
  50.6 0.7 %finish.1 = (f32[4,6]{1,0:T(4,128)}, f32[1,1]{1,0:T(1,128)}) custom-call(f32[56,128]{1,0:T(8,128)S(1)} %collective-permute-done.5.first, f32[56,128]{1,0:T(8,128)S(1)} %collective-permute-done.6.second), custom_call_target="tpu_custom_call" | custom-call | tf_op jit(solution)/shard_map/finish/pallas_call | solution.py:379
Async XLA Ops:
  0.6 7.7 %collective-permute-start = (f32[4,6]{1,0:T(4,128)}, f32[4,6]{1,0:T(4,128)S(1)}, u32[]{:S(2)}, u32[]{:S(2)}) collective-permute-start(f32[4,6]{1,0:T(4,128)} %param.13), channel_id=1, source_target_pairs={{0,0},{25,1},{2,2},{17,3},{4,4},{9,5},{6,6},{1,7},{8,8},{27,9},{10... | collective-permute-start | bytes 296 | tf_op jit(solution)/shard_map/ppermute | solution.py:291
  17.1 5.3 %collective-permute-start.1 = (f32[256,256]{1,0:T(8,128)S(1)}, f32[256,256]{1,0:T(8,128)S(1)}, u32[]{:S(2)}, u32[]{:S(2)}) collective-permute-start(f32[256,256]{1,0:T(8,128)S(1)} %get-tuple-element.27.segment.held), channel_id=1, source_target_pairs={{0,2},{2,0},{4,6},{6,4},{8,10},{10,8},{12,14},{14,12},{16,18},{18,... | collective-permute-start | bytes 786440 | tf_op jit(solution)/shard_map/ppermute | solution.py:333
  22.8 13.8 %copy-start = (f32[256,256]{1,0:T(8,128)S(1)}, f32[256,256]{1,0:T(8,128)}, u32[]{:S(2)}) copy-start(f32[256,256]{1,0:T(8,128)} %target.1) | copy-start | bytes 786436
  22.8 7.2 %collective-permute-start.2 = (f32[256,256]{1,0:T(8,128)S(1)}, f32[256,256]{1,0:T(8,128)S(1)}, u32[]{:S(2)}, u32[]{:S(2)}) collective-permute-start(f32[256,256]{1,0:T(8,128)S(1)} %join.3.held), channel_id=1, source_target_pairs={{0,4},{2,6},{4,0},{6,2},{8,12},{10,14},{12,8},{14,10},{16,20},{18,... | collective-permute-start | bytes 786440 | tf_op jit(solution)/shard_map/ppermute | solution.py:333
  30.4 5.3 %collective-permute-start.3 = (f32[256,256]{1,0:T(8,128)S(1)}, f32[256,256]{1,0:T(8,128)S(1)}, u32[]{:S(2)}, u32[]{:S(2)}) collective-permute-start(f32[256,256]{1,0:T(8,128)S(1)} %join.4.held), channel_id=1, source_target_pairs={{0,8},{2,10},{4,12},{6,14},{8,0},{10,2},{12,4},{14,6},{16,24},{18,... | collective-permute-start | bytes 786440 | tf_op jit(solution)/shard_map/ppermute | solution.py:333
  36.1 5.6 %collective-permute-start.4 = (f32[256,256]{1,0:T(8,128)S(1)}, f32[256,256]{1,0:T(8,128)S(1)}, u32[]{:S(2)}, u32[]{:S(2)}) collective-permute-start(f32[256,256]{1,0:T(8,128)S(1)} %join.5), channel_id=1, source_target_pairs={{0,24},{2,26},{4,28},{6,30},{8,16},{10,18},{12,20},{14,22},{16,8},... | collective-permute-start | bytes 786440 | tf_op jit(solution)/shard_map/ppermute | solution.py:333
  44.1 6.4 %collective-permute-start.6 = (f32[56,128]{1,0:T(8,128)S(1)}, f32[56,128]{1,0:T(8,128)S(1)}, u32[]{:S(2)}, u32[]{:S(2)}) collective-permute-start(f32[56,128]{1,0:T(8,128)S(1)} %gradient.1), channel_id=1, source_target_pairs={{1,25},{3,17},{5,9},{7,1},{9,27},{11,19},{13,11},{15,3},{17,29},{1... | collective-permute-start | bytes 86024 | tf_op jit(solution)/shard_map/ppermute | solution.py:376
  46.1 4.5 %collective-permute-start.5 = (f32[56,128]{1,0:T(8,128)S(1)}, f32[56,128]{1,0:T(8,128)S(1)}, u32[]{:S(2)}, u32[]{:S(2)}) collective-permute-start(f32[56,128]{1,0:T(8,128)S(1)} %gradient.1), channel_id=1, source_target_pairs={{1,24},{3,16},{5,8},{7,0},{9,26},{11,18},{13,10},{15,2},{17,28},{1... | collective-permute-start | bytes 86024 | tf_op jit(solution)/shard_map/ppermute | solution.py:376
